TPU v7x, 256 devices: a whole 4x4x8 slice. The times are simulated.
256 devices in a mesh: occ: 4 (over z_hi), vir: 64 (over y, z_lo, x, core).
Axes of the slice: x: 4, y: 4, z: 8 (z_hi: 4, z_lo: 2; z = z_hi * 2 + z_lo), core: 2. Of those that a mesh axis runs over, the one named last changes fastest.
Arguments:
- amplitudes: float32 [49152, 1024], P('vir', 'occ'), may hold values from -6 to 6
- integrals: float32 [768, 327680], P('occ', 'vir'), may hold values from -0.21875 to 0.21875
- eps_vir: float32 [327680], P('vir'), may hold values from 0.5 to 3
- eps_occ: float32 [1024], P('occ'), may hold values from -2 to -0.5
- panel_owner: int32 [12], replicated, may hold values from 0 to 63
- block_target: int32 [4096], replicated, may hold values from 0 to 4095, as said below
Outputs:
- ladder_tiles: float32 [327680, 1024], P('vir', 'occ')
Inputs may be any that keep to these rules, and one draw needn't show every extreme that they name: block_target is a permutation. The 64 blocks of each index of vir go to 32 owner indices, exactly 2 to each, and each owner receives exactly 2 blocks from each of 32 senders; block b of the whole lies on index b // 64.
All inputs are finite; a program needn't handle non-finite values.
Results may differ from a plain program's by a relative error of at most 0.000082.
Values sent between devices are 32-bit elements; how exact they have to be, the bound alone decides.
A program may use at most 128 MiB of HBM per device.

v0:
```python
import jax
import jax.numpy as jnp
from jax import lax
from jax.sharding import PartitionSpec as P

STEPS = 12
NB_DEV = 64


highest = lax.Precision.HIGHEST


def broadcast(block, axis, holder):
    block = jnp.where(lax.axis_index(axis) == holder, block, jnp.zeros_like(block))
    return lax.psum(block, axis)


def block_ranks(block_target, blocks_dev):
    senders = block_target.shape[0] // blocks_dev
    owners = (block_target // blocks_dev).reshape(senders, blocks_dev)
    positions = jnp.arange(blocks_dev)
    earlier = (owners[:, :, None] == owners[:, None, :]) & (
        positions[None, None, :] < positions[None, :, None]
    )
    return (owners, jnp.sum(earlier.astype(jnp.int32), axis=2))


def arrivals(block_target, slot_rank, blocks_dev, device_id):
    wanted = device_id * blocks_dev + jnp.arange(blocks_dev)
    matches = (block_target[None, :] == wanted[:, None]).astype(jnp.int32)
    source_block = jnp.sum(matches * jnp.arange(block_target.shape[0])[None, :], axis=1)
    return (source_block // blocks_dev, jnp.take(slot_rank.reshape(-1), source_block))


def pack(blocks, owner_list, rank_list, senders, capacity):
    buffer = jnp.zeros((senders, capacity) + blocks.shape[1:], blocks.dtype)
    return buffer.at[owner_list, rank_list].set(blocks)


def local(amplitudes, integrals, eps_vir, eps_occ, panel_owner, block_target):
    device_id = lax.axis_index("vir")
    senders = lax.axis_size("vir")
    blocks_dev = NB_DEV
    capacity = max(2, 2 * blocks_dev // senders)
    col_count = eps_vir.shape[0]
    block_cols = col_count // blocks_dev
    panel_rows = amplitudes.shape[0] // STEPS
    pieces = []
    for step_index in range(STEPS):
        own_rows = amplitudes[step_index * panel_rows : (step_index + 1) * panel_rows]
        pieces.append(broadcast(own_rows, "vir", panel_owner[step_index]))
    panels = jnp.concatenate(pieces, 0)
    owners, slot_rank = block_ranks(block_target, blocks_dev)
    senders_of, arrival_rank = arrivals(block_target, slot_rank, blocks_dev, device_id)
    ladder = lax.dot_general(
        lax.all_gather(integrals, "occ", axis=0, tiled=True),
        panels,
        (((0,), (0,)), ((), ())),
        precision=highest,
        preferred_element_type=jnp.float32,
    )
    scaled = ladder / (eps_vir[:, None] - eps_occ[None, :])
    blocks = scaled.reshape(blocks_dev, block_cols, scaled.shape[1])
    buffer = pack(blocks, owners[device_id], slot_rank[device_id], senders, capacity)
    arrived = lax.all_to_all(buffer, "vir", split_axis=0, concat_axis=0, tiled=True)
    return arrived[senders_of, arrival_rank].reshape(col_count, scaled.shape[1])


def solution(mesh):
    in_specs = (P("vir", "occ"), P("occ", "vir"), P("vir"), P("occ"), P(), P())
    out_specs = P("vir", "occ")
    return jax.shard_map(local, mesh=mesh, in_specs=in_specs, out_specs=out_specs, check_vma=False)
```

profile of v0, /device:TPU:1, one launch (start us, length us, event | category | flops | bytes accessed | tf_op | source)
XLA Modules:
  0.0 1018.6 jit_solution(14401535388239601117)
XLA Ops:
  7.4 0.0 copy-start
  7.4 0.0 copy-start.2
  7.4 0.0 copy-start.1
  7.4 0.0 all-reduce.3.cloned.1.call-start
  7.4 1.8 fusion.12
  16.6 1.6 slice_select_fusion.1
  18.2 1.9 slice_select_fusion
  20.2 0.0 all-reduce.3.cloned.1.call-update
  20.2 0.0 all-gather.2.cloned.1.call-start
  20.2 0.5 all-gather.2.cloned.1.call-update
  20.8 0.0 copy-done
  20.8 0.1 reshape.194
  20.9 1.9 convert_reduce_fusion
  22.8 784.0 %all-reduce.3.cloned.1.call-done = (f32[64,256]{1,0:T(8,128)}, f32[64,256]{1,0:T(8,128)}, f32[64,256]{1,0:T(8,128)}, f32[64,256]{1,0:T(8,128)}, f32[64,256]{1,0:...) async-done(((f32[64,256]{1,0:T(8,128)}, f32[64,256]{1,0:T(8,128)}, ...) | async-done | bytes 786448 | tf_op jit(solution)/shard_map/psum | solution.py:15
  806.8 0.8 constant_dynamic-update-slice_fusion.11
  807.6 0.8 constant_dynamic-update-slice_fusion.10
  808.5 0.8 constant_dynamic-update-slice_fusion.9
  809.3 0.8 constant_dynamic-update-slice_fusion.8
  810.2 0.8 constant_dynamic-update-slice_fusion.7
  811.0 0.8 constant_dynamic-update-slice_fusion.6
  811.8 0.8 constant_dynamic-update-slice_fusion.5
  812.7 0.8 constant_dynamic-update-slice_fusion.4
  813.5 0.8 constant_dynamic-update-slice_fusion.3
  814.4 0.8 constant_dynamic-update-slice_fusion.2
  815.2 0.8 constant_dynamic-update-slice_fusion.1
  816.1 0.8 constant_dynamic-update-slice_fusion
  816.9 0.0 all-gather.2.cloned.1.call-done
  816.9 0.0 copy-done.2
  816.9 0.0 copy-done.1
  816.9 18.8 %fusion = f32[5120,256]{0,1:T(8,128)} fusion(f32[768,256]{1,0:T(8,128)S(1)} %constant_dynamic-update-slice_fusion, f32[768,5120]{1,0:T(8,128)} %all-gather.2.cloned.1.call-done, f32[256]{0:T(256)S(1)} %copy-done.2, f32[5120]{0:T(1024)S(1)} %copy-done.1), kind=kOutput, calls=%fused_computation.4 | convolution fusion | flops 12082216960 | bytes 21779456 | tf_op jit(solution)/shard_map/dot_general | solution.py:55
  835.8 5.9 copy.8
  841.6 5.3 broadcast_in_dim.6
  846.9 13.8 %scatter_fusion = f32[64,2,80,256]{3,2,1,0:T(8,128)} fusion(f32[64,2,80,256]{3,2,1,0:T(8,128)} %broadcast_in_dim.6, s32[64]{0:T(128)S(1)} %fusion.10, f32[64,80,256]{2,1,0:T(8,128)} %bitcast.58), kind=kCustom, calls=%fused_computation.2 | custom fusion | bytes 15729152 | tf_op jit(solution)/shard_map/scatter | solution.py:37
  860.7 7.1 all-to-all-start
  867.8 0.1 reshape.196
  867.9 0.3 select_reduce_fusion
  868.2 0.8 gather_fusion
  869.0 135.0 %all-to-all-done = f32[64,2,80,256]{3,2,1,0:T(8,128)} async-done(((f32[64,2,80,256]{3,2,1,0:T(8,128)}), f32[64,2,80,256]{3,2,1,0:T(8,128)}, u32[]{:S(2)}, u32[]{:S(2)}) %all-to-all-start) | async-done | bytes 10485792 | tf_op jit(solution)/shard_map/all_to_all | solution.py:65
  1004.0 7.2 gather_fusion.1
  (7 shorter events, 0.1 us)
Async XLA Ops:
  7.4 13.4 %copy-start = (s32[4096]{0:T(1024)S(1)}, s32[4096]{0:T(1024)}, u32[]{:S(2)}) copy-start(s32[4096]{0:T(1024)} %param.11) | copy-start | bytes 49156
  7.4 809.5 %copy-start.2 = (f32[256]{0:T(256)S(1)}, f32[256]{0:T(256)}, u32[]{:S(2)}) copy-start(f32[256]{0:T(256)} %param.9) | copy-start | bytes 3076
  7.4 809.6 %copy-start.1 = (f32[5120]{0:T(1024)S(1)}, f32[5120]{0:T(1024)}, u32[]{:S(2)}) copy-start(f32[5120]{0:T(1024)} %param.8) | copy-start | bytes 61444
  7.4 799.4 %all-reduce.3.cloned.1.call-start = ((), (), s32[]{:S(2)}) async-start(), calls=%async_computation.2 | async-start | bytes 1572864 | tf_op jit(solution)/shard_map/psum | solution.py:15
  20.2 796.7 %all-gather.2.cloned.1.call-start = ((), (), s32[]{:S(2)}) async-start(), calls=%async_computation.1 | async-start | bytes 19660800 | tf_op jit(solution)/shard_map/all_gather | solution.py:56
  860.7 143.3 %all-to-all-start = ((f32[64,2,80,256]{3,2,1,0:T(8,128)}), f32[64,2,80,256]{3,2,1,0:T(8,128)}, u32[]{:S(2)}, u32[]{:S(2)}) async-start(f32[64,2,80,256]{3,2,1,0:T(8,128)} %scatter_fusion), calls=%async_computation | async-start | bytes 20971520 | tf_op jit(solution)/shard_map/all_to_all | solution.py:65
Sparse Core Ops, SparseCore 0:
  20.3 786.4 all-reduce.2
Sparse Core Ops, SparseCore 1:
  22.5 281.5 all-gather.1
where the time goes:
time: 1020 us
  waiting for transfers between devices  920 us (90%)
  local copies, waits for them, and re-layouts  45 us (4%)
  between operations  22.4 us (2%)
  matrix products  18.8 us (2%)
    psum x1, waiting for transfers between devices, broadcast(): return lax.psum(block, axis)  784 us
    all_to_all x1, waiting for transfers between devices, local(): lax.all_to_all(buffer, 'vir', split_axis=0, concat_axis=0, tiled=True)  135 us
  transfers between devices with their start and end apart: 3, of which 2 were waited for; matrix products, arithmetic and copies ran while one was open for 1% of the time, Pallas kernels for 0%

commit v1 on v0

v1 whole, which is shorter than its diff:
```python
import functools

import jax
import jax.numpy as jnp
from jax import lax
from jax.experimental import pallas as pl
from jax.experimental.pallas import tpu as pltpu
from jax.sharding import PartitionSpec as P

MESH = pl.DeviceIdType.MESH
STEPS = 12
N_OCC = 4
DIGITS = ((1, 2), (2, 4), (8, 2), (16, 4))


def remote(src, dst, sems, k, peer):
    send, recv = sems
    return pltpu.make_async_remote_copy(
        src_ref=src, dst_ref=dst, send_sem=send.at[k], recv_sem=recv.at[k], device_id=peer, device_id_type=MESH
    )


def gcd16(n):
    g = 16
    while n % g:
        g //= 2
    return g


def panel_kernel(digits, per_step, owner_ref, amp_ref, out_ref, *scratch):
    levels = len(digits)
    arrived, kept, transit = scratch[:levels], scratch[levels : 2 * levels - 1], scratch[2 * levels - 1]
    sems = scratch[2 * levels :]
    occ, vir = lax.axis_index("occ"), lax.axis_index("vir")
    mine = [(vir // stride) % size for stride, size in digits]

    def along(level, digit):
        stride, _ = digits[level]
        return (occ, vir + (digit - mine[level]) * stride)

    up, down = (lax.rem(occ + 1, N_OCC), vir), (lax.rem(occ + N_OCC - 1, N_OCC), vir)
    far = lax.rem(occ + 2, N_OCC)
    peers = [up, down]
    for level, (_, size) in enumerate(digits):
        peers += [along(level, lax.rem(mine[level] + d, size)) for d in range(1, size)]
    barrier = pltpu.get_barrier_semaphore()
    for peer in peers:
        pl.semaphore_signal(barrier, inc=1, device_id=peer, device_id_type=MESH)
    pl.semaphore_wait(barrier, len(peers))

    k = 0
    started = []
    current, base, bases, lengths = amp_ref, 0, [], []
    length = amp_ref.shape[0]
    for level, (stride, size) in enumerate(digits):
        part = length // size
        copies = []
        for d in range(1, size):
            digit = lax.rem(mine[level] + d, size)
            copies.append(
                remote(current.at[pl.ds(digit * part, part)], arrived[level].at[d - 1], sems, k, along(level, digit))
            )
            k += 1
        for copy in copies:
            copy.start()
        offset = mine[level] * part
        base = base + offset
        target, target_base = (kept[level], 0) if level < levels - 1 else (out_ref.at[occ], base)
        for copy in copies:
            copy.wait_recv()
        group = min(gcd16(part), per_step)
        for g in range(part // group):
            holder = owner_ref[(base + g * group) // per_step]
            digit = (holder // stride) % size
            value = current[pl.ds(offset + g * group, group)]
            for d in range(1, size):
                source = lax.rem(mine[level] + size - d, size)
                value = jnp.where(digit == source, arrived[level][d - 1, pl.ds(g * group, group)], value)
            target[pl.ds(target_base + g * group, group)] = value
        started += copies
        current, length = (target, part)
        bases.append(base)
        lengths.append(part)

    for level in range(levels - 1, 0, -1):
        piece = out_ref.at[occ, pl.ds(bases[level], lengths[level])]
        copies = []
        for d in range(1, digits[level][1]):
            digit = lax.rem(mine[level] + d, digits[level][1])
            copies.append(remote(piece, piece, sems, k, along(level, digit)))
            k += 1
        for copy in copies:
            copy.start()
        for copy in copies:
            copy.wait_recv()
        started += copies

    half = lengths[0]
    quarter = half // 2
    sibling = along(0, 1 - mine[0])
    above, below = lax.rem(occ + 1, N_OCC), lax.rem(occ + N_OCC - 1, N_OCC)

    def rows(which, start, size):
        return out_ref.at[which, pl.ds(bases[0] + start, size)]

    own = rows(occ, 0, half)
    first = [
        remote(own, own, sems, k, up),
        remote(own, own, sems, k + 1, down),
        remote(rows(occ, 0, quarter), transit.at[0], sems, k + 2, up),
        remote(rows(occ, quarter, quarter), transit.at[1], sems, k + 3, down),
    ]
    relays = [
        remote(transit.at[0], rows(below, 0, quarter), sems, k + 4, up),
        remote(transit.at[1], rows(above, quarter, quarter), sems, k + 5, down),
    ]
    k += 6
    order = [first[2], first[3], first[0], first[1]]
    for copy in order:
        copy.start()
    shares = [remote(rows(which, 0, half), rows(which, 0, half), sems, k + n, sibling)
              for n, which in enumerate((occ, below, above, far))]
    shares[0].start()
    for n in range(2):
        first[2 + n].wait_recv()
        relays[n].start()
    for n in range(2):
        first[n].wait_recv()
        shares[1 + n].start()
    for n in range(2):
        relays[n].wait_recv()
    shares[3].start()
    for copy in shares:
        copy.wait_recv()
    for copy in started + first + relays + shares:
        copy.wait_send()


def broadcast_panels(amplitudes, panel_owner, digits):
    rows, cols = amplitudes.shape
    units = (rows // 8) * (cols // 128)
    amps = amplitudes.reshape(rows // 8, 8, cols // 128, 128).transpose(0, 2, 1, 3).reshape(units, 8, 128)
    per_step = units // STEPS
    arrived, kept, length, count = [], [], units, 0
    for level, (_, size) in enumerate(digits):
        length //= size
        arrived.append(pltpu.VMEM((size - 1, length, 8, 128), jnp.float32))
        kept.append(pltpu.VMEM((length, 8, 128), jnp.float32))
        count += (size - 1) * (2 if level else 1)
    half = units // digits[0][1]
    count += 10
    out = pl.pallas_call(
        functools.partial(panel_kernel, digits, per_step),
        out_shape=jax.ShapeDtypeStruct((N_OCC, units, 8, 128), jnp.float32),
        in_specs=[pl.BlockSpec(memory_space=pltpu.SMEM), pl.BlockSpec(memory_space=pltpu.VMEM)],
        out_specs=pl.BlockSpec(memory_space=pltpu.VMEM),
        scratch_shapes=arrived
        + kept[:-1]
        + [
            pltpu.VMEM((2, half // 2, 8, 128), jnp.float32),
            pltpu.SemaphoreType.DMA((count,)),
            pltpu.SemaphoreType.DMA((count,)),
        ],
        compiler_params=pltpu.CompilerParams(collective_id=0, has_side_effects=True),
        name="panels",
    )(panel_owner, amps)
    out = out.reshape(N_OCC, rows // 8, cols // 128, 8, 128).transpose(1, 3, 0, 2, 4)
    return out.reshape(rows, N_OCC * cols)


AHEAD = 3


def ladder_kernel(x_ref, high_ref, low_ref, out_ref, held, passing, result, passing_result, send, recv, own_sem):
    chunks = held.shape[1]
    rows, lanes = held.shape[2], held.shape[3]
    width = out_ref.shape[2]
    half, cols = rows // 2, out_ref.shape[1]
    block = cols // 2
    occ, vir = lax.axis_index("occ"), lax.axis_index("vir")
    above, below, far = (lax.rem(occ + n, N_OCC) for n in (1, N_OCC - 1, 2))
    up, down = (above, vir), (below, vir)

    barrier = pltpu.get_barrier_semaphore()
    for peer in (up, down):
        pl.semaphore_signal(barrier, inc=1, device_id=peer, device_id_type=MESH)
    pl.semaphore_wait(barrier, 2)

    def copy(kind, j):
        make = lambda src, dst, peer: pltpu.make_async_remote_copy(
            src_ref=src, dst_ref=dst, send_sem=send.at[kind, j], recv_sem=recv.at[kind, j], device_id=peer,
            device_id_type=MESH,
        )
        if kind == 0:
            return make(x_ref.at[far * chunks + j, pl.ds(0, half)], passing.at[0, j], up)
        if kind == 1:
            return make(x_ref.at[far * chunks + j, pl.ds(half, half)], passing.at[1, j], down)
        if kind == 2:
            return make(x_ref.at[above * chunks + j], held.at[occ, j], up)
        if kind == 3:
            return make(x_ref.at[below * chunks + j], held.at[occ, j], down)
        if kind == 4:
            return make(passing.at[0, j], held.at[below, j, pl.ds(0, half)], up)
        if kind == 5:
            return make(passing.at[1, j], held.at[above, j, pl.ds(half, half)], down)
        if kind == 6:
            return make(result.at[j, far, pl.ds(0, block)], passing_result.at[0, j], up)
        if kind == 7:
            return make(result.at[j, far, pl.ds(block, block)], passing_result.at[1, j], down)
        if kind == 8:
            return make(result.at[j, above], out_ref.at[occ * chunks + j], up)
        if kind == 9:
            return make(result.at[j, below], out_ref.at[occ * chunks + j], down)
        if kind == 10:
            return make(passing_result.at[0, j], out_ref.at[below * chunks + j, pl.ds(0, block)], up)
        return make(passing_result.at[1, j], out_ref.at[above * chunks + j, pl.ds(block, block)], down)

    own_copy = pltpu.make_async_copy(x_ref.at[pl.ds(occ * chunks, chunks)], held.at[occ], own_sem)
    own_copy.start()

    def send_chunk(j):
        for kind in range(4):
            copy(kind, j).start()

    def first(j, _):
        send_chunk(j)
        return 0

    lax.fori_loop(0, AHEAD, first, 0)
    own_copy.wait()

    def compute(j):
        low_lane = lax.broadcasted_iota(jnp.int32, (block, lanes), 1) < lanes // 2
        tiles = [held[n, j, pl.ds(0, cols)] for n in range(N_OCC)]
        folds = [held[n, j, pl.ds(cols, block)] for n in range(N_OCC)]
        for n in range(0, N_OCC, 2):
            left, right = folds[n], folds[n + 1]
            one = jnp.where(low_lane, left, pltpu.roll(right, lanes // 2, 1))
            two = jnp.where(low_lane, pltpu.roll(left, lanes // 2, 1), right)
            tiles.append(jnp.concatenate([one, two], axis=0))
        whole = jnp.concatenate(tiles, axis=1)
        high = whole.astype(jnp.bfloat16)
        low = (whole - high.astype(jnp.float32)).astype(jnp.bfloat16)
        for n in range(N_OCC):
            at = slice(n * width, (n + 1) * width)
            dot = lambda a, b: jnp.dot(a, b, preferred_element_type=jnp.float32)
            result[j, n] = (
                dot(high, low_ref[:, at]) + dot(low, high_ref[:, at])
            ) + dot(high, high_ref[:, at])
        out_ref[occ * chunks + j] = result[j, occ]

    def step(t, _):
        @pl.when(t + AHEAD < chunks)
        def _():
            send_chunk(t + AHEAD)

        @pl.when(t < chunks)
        def _():
            for kind in range(2):
                copy(kind, t).wait_recv()
                copy(4 + kind, t).start()

        @pl.when((t >= 2) & (t < chunks + 2))
        def _():
            for kind in range(6, 10):
                copy(kind, t - 2).start()

        @pl.when((t >= 1) & (t < chunks + 1))
        def _():
            for kind in range(2, 6):
                copy(kind, t - 1).wait_recv()
            compute(t - 1)

        @pl.when(t >= 3)
        def _():
            for kind in range(2):
                copy(6 + kind, t - 3).wait_recv()
                copy(10 + kind, t - 3).start()

        return 0

    lax.fori_loop(0, chunks + 3, step, 0)

    def last(j, _):
        for kind in range(8, 12):
            copy(kind, j).wait_recv()
        for kind in range(12):
            copy(kind, j).wait_send()
        return 0

    lax.fori_loop(0, chunks, last, 0)


def ladder_of(x, high, low):
    pairs, rows, lanes = x.shape
    chunks = pairs // N_OCC
    width = high.shape[1] // N_OCC
    cols = rows * 2 // 3
    vmem = pl.BlockSpec(memory_space=pltpu.VMEM)
    return pl.pallas_call(
        ladder_kernel,
        out_shape=jax.ShapeDtypeStruct((pairs, cols, width), jnp.float32),
        in_specs=[vmem] * 3,
        out_specs=vmem,
        scratch_shapes=[
            pltpu.VMEM((N_OCC, chunks, rows, lanes), jnp.float32),
            pltpu.VMEM((2, chunks, rows // 2, lanes), jnp.float32),
            pltpu.VMEM((chunks, N_OCC, cols, width), jnp.float32),
            pltpu.VMEM((2, chunks, cols // 2, width), jnp.float32),
            pltpu.SemaphoreType.DMA((12, chunks)),
            pltpu.SemaphoreType.DMA((12, chunks)),
            pltpu.SemaphoreType.DMA,
        ],
        compiler_params=pltpu.CompilerParams(collective_id=1, has_side_effects=True),
        name="ladder",
    )(x, high, low)


def split(value):
    high = lax.reduce_precision(value, 8, 7)
    return high.astype(jnp.bfloat16), (value - high).astype(jnp.bfloat16)


def local(amplitudes, integrals, eps_vir, eps_occ, panel_owner, block_target):
    me = lax.axis_index("vir")
    senders = lax.axis_size("vir")
    depth, col_count = integrals.shape
    blocks_dev = block_target.shape[0] // senders
    block = col_count // blocks_dev
    lanes = 128

    owners = block_target.reshape(senders, blocks_dev) // blocks_dev
    position = jnp.arange(blocks_dev, dtype=jnp.int32)
    goes = lax.dynamic_index_in_dim(owners, me, 0, keepdims=False)[None, :] == jnp.arange(senders)[:, None]
    first = jnp.min(jnp.where(goes, position[None, :], blocks_dev - 1), axis=1)
    second = jnp.max(jnp.where(goes, position[None, :], 0), axis=1)

    comes = owners == me
    sends = jnp.any(comes, axis=1)
    order = jnp.arange(senders, dtype=jnp.int32)
    rank = jnp.sum((sends[None, :] & (order[None, :] < order[:, None])).astype(jnp.int32), axis=1)
    pair_of = jnp.arange(senders // 2, dtype=jnp.int32)
    sender_of = jnp.sum(
        jnp.where(sends[None, :] & (rank[None, :] == pair_of[:, None]), order[None, :], 0), axis=1
    )
    lead = jnp.min(jnp.where(comes, position[None, :], blocks_dev), axis=1)
    place = 2 * rank[:, None] + (position[None, :] != lead[:, None]).astype(jnp.int32)
    wanted = me * blocks_dev + position
    found = block_target.reshape(1, senders, blocks_dev) == wanted[:, None, None]
    source = jnp.sum(jnp.where(found, place[None], 0), axis=(1, 2))

    turned = integrals.T.reshape(blocks_dev, block, depth)
    one, two = turned[first], turned[second]
    energies = eps_vir.reshape(blocks_dev, block)
    sent_eps = jnp.concatenate([energies[first], energies[second]], axis=1)
    sent_eps = jnp.pad(sent_eps, ((0, 0), (0, 8 * lanes - 2 * block))).reshape(senders, 8, lanes)
    packed = jnp.concatenate(
        [one[:, :, :lanes], two[:, :, :lanes], jnp.concatenate([one[:, :, lanes:], two[:, :, lanes:]], 2), sent_eps], 1
    )
    arrived = lax.all_to_all(packed, "vir", split_axis=0, concat_axis=0, tiled=True)

    panels = broadcast_panels(amplitudes, panel_owner, DIGITS)
    pieces = panels.reshape(N_OCC, depth, panels.shape[1])
    ordered = jnp.concatenate(
        [pieces[:, :lanes].reshape(-1, panels.shape[1]), pieces[:, lanes:].reshape(-1, panels.shape[1])], 0
    )
    high, low = split(ordered)

    compact = arrived[sender_of]
    rows = 3 * block
    ladder = ladder_of(compact[:, :rows], high, low)
    ladder = ladder.reshape(blocks_dev, block, ladder.shape[2])
    eps = compact[:, rows:].reshape(senders // 2, 8 * lanes)[:, : 2 * block].reshape(blocks_dev, block)
    scaled = ladder[source] / (eps[source][:, :, None] - eps_occ[None, None, :])
    return scaled.reshape(col_count, ladder.shape[2])


def solution(mesh):
    in_specs = (P("vir", "occ"), P("occ", "vir"), P("vir"), P("occ"), P(), P())
    out_specs = P("vir", "occ")
    return jax.shard_map(local, mesh=mesh, in_specs=in_specs, out_specs=out_specs, check_vma=False)
```

time: 1020 us -> 443 us (0.43)
  waiting for transfers between devices: 920 us -> 0.01 us
  Pallas kernels: 0 us -> 373 us
  between operations: 22.4 us -> 0.19 us
  matrix products: 18.8 us -> 0 us
    psum x1 -> x0, waiting for transfers between devices: 784 us -> none  [broadcast(): return lax.psum(block, axis)]
    pallas_call x0 -> x2, Pallas kernels: none -> 373 us  [the longest x1 209 us: ladder_of(): pl.pallas_call(ladder_kernel, out_shape=jax.ShapeDtypeStruct((pairs, cols...]
    all_to_all x1, waiting for transfers between devices: 135 us -> 0.01 us  [local(): lax.all_to_all(packed, 'vir', split_axis=0, concat_axis=0, tiled=True)]
    dot_general x1 -> x0, matrix products: 18.8 us -> none  [local(): lax.dot_general(lax.all_gather(integrals, 'occ', axis=0, tiled=True), pan...]
    gather x2 -> x7, local copies, waits for them, and re-layouts: 7.99 us -> 25 us  [the longest x2 11.4 us: local(): one, two = (turned[first], turned[second])]
    scatter x1 -> x0, local copies, waits for them, and re-layouts: 13.8 us -> none  [pack(): return buffer.at[owner_list, rank_list].set(blocks)]
  transfers between devices with their start and end apart: 3 -> 1, of which waited for: 2 -> 0; matrix products, arithmetic and copies ran while one was open for 1% -> 2% of each run, Pallas kernels for 0% -> 37%
where the time goes in v1:
time: 443 us; the launch traced here: 441 us
  Pallas kernels  373 us (84%)
  local copies, waits for them, and re-layouts  43.2 us (10%)
  other arithmetic  13.9 us (3%)
  starting transfers between devices  10.5 us (2%)
    pallas_call x1, Pallas kernels, ladder_of(): pl.pallas_call(ladder_kernel, out_shape=jax.ShapeDtypeStruct((pairs, cols...  209 us
    pallas_call x1, Pallas kernels, broadcast_panels(): pl.pallas_call(functools.partial(panel_kernel, digits, per_step), out_sha...  164 us
    gather x2, local copies, waits for them, and re-layouts, local(): one, two = (turned[first], turned[second])  11.4 us
    all_to_all x1, starting transfers between devices, local(): lax.all_to_all(packed, 'vir', split_axis=0, concat_axis=0, tiled=True)  10.5 us
  transfers between devices with their start and end apart: 1, of which 0 were waited for; matrix products, arithmetic and copies ran while one was open for 2% of the time, Pallas kernels for 37%

profile of v1, /device:TPU:1, one launch (start us, length us, event | category | flops | bytes accessed | tf_op | source)
XLA Modules:
  0.0 441.2 jit_solution(4247929975191450380)
XLA Ops:
  0.0 0.8 reshape.139
  0.8 0.1 select_reduce_fusion.1
  0.9 0.1 select_reduce_fusion.3
  1.1 0.8 reshape.140
  1.9 0.6 gather_fusion.2
  2.5 0.6 gather_fusion.3
  3.1 5.6 %copy.11 = f32[192,5120]{0,1:T(8,128)} copy(f32[192,5120]{1,0:T(8,128)} %param.7) | data formatting | bytes 7864320 | tf_op args[1]
  8.7 5.7 %gather_fusion = f32[64,80,192]{2,1,0:T(8,128)} fusion(f32[64,80,192]{2,1,0:T(8,128)} %bitcast.42, s32[1024]{0:T(1024)S(1)} %pad_clamp_fusion.3), kind=kCustom, calls=%fused_computation | custom fusion | bytes 7864576 | tf_op jit(solution)/shard_map/gather | solution.py:353
  14.4 5.7 %gather_fusion.1 = f32[64,80,192]{2,1,0:T(8,128)} fusion(f32[64,80,192]{2,1,0:T(8,128)} %bitcast.43, s32[1024]{0:T(1024)S(1)} %pad_clamp_fusion.2), kind=kCustom, calls=%fused_computation.1 | custom fusion | bytes 7864576 | tf_op jit(solution)/shard_map/gather | solution.py:353
  20.1 0.0 slice-start
  20.1 0.0 slice-start.1
  20.1 0.0 slice-start.2
  20.1 0.0 slice-start.3
  20.1 0.1 fusion.1
  20.2 1.6 slice-done
  21.8 0.8 slice-done.1
  22.6 0.8 slice-done.2
  23.4 0.7 slice-done.3
  24.1 3.9 pad_maximum_fusion
  28.1 10.5 %all-to-all-start = ((f32[64,248,128]{2,1,0:T(8,128)}), f32[64,248,128]{2,1,0:T(8,128)}, u32[]{:S(2)}, u32[]{:S(2)}) async-start(f32[64,248,128]{2,1,0:T(8,128)} %pad_maximum_fusion), calls=%async_computation | async-start | bytes 16252928 | tf_op jit(solution)/shard_map/all_to_all | solution.py:360
  38.6 164.2 %panels.1 = f32[4,192,8,128]{3,2,1,0:T(8,128)} custom-call(s32[12]{0:T(128)} %owner_ref.1, f32[192,8,128]{2,1,0:T(8,128)} %bitcast.52), custom_call_target="tpu_custom_call" | custom-call | tf_op jit(solution)/shard_map/panels/pallas_call | solution.py:152
  202.7 2.4 copy.12
  205.1 0.1 slice.55
  205.2 0.1 slice.56
  205.3 0.1 reduce_or.9
  205.5 0.1 convert_reduce_fusion
  205.6 0.1 select_reduce_fusion.4
  205.7 0.1 convert_add_fusion
  205.8 1.4 select_reduce_fusion
  207.2 2.3 fusion
  209.5 0.0 all-to-all-done
  209.5 6.1 %gather_fusion.4 = f32[32,248,128]{2,1,0:T(8,128)} fusion(f32[64,248,128]{2,1,0:T(8,128)} %all-to-all-done, s32[1024]{0:T(1024)S(1)} %pad_clamp_fusion.1), kind=kCustom, calls=%fused_computation.4 | custom fusion | bytes 8126592 | tf_op jit(solution)/shard_map/gather | solution.py:369
  215.6 0.0 slice-start.4
  215.6 4.4 slice.54.x_ref
  220.0 0.0 slice-done.4
  220.0 0.1 reshape.149
  220.1 209.2 %ladder.1 = f32[32,160,256]{2,1,0:T(8,128)} custom-call(f32[32,240,128]{2,1,0:T(8,128)} %slice.54.x_ref, bf16[768,1024]{1,0:T(8,128)(2,1)} %get-tuple-element.11.high_ref, bf16[768,1024]{1,0:T(8,128)(2,1)} %get-tuple-element.10.low_ref), custom_call_target="tpu_custom_call" | custom-call | tf_op jit(solution)/shard_map/ladder/pallas_call | solution.py:300
  429.3 0.0 copy-start
  429.4 5.7 %gather_fusion.5 = f32[64,80,256]{2,1,0:T(8,128)} fusion(f32[64,80,256]{2,1,0:T(8,128)} %bitcast.44, s32[1024]{0:T(1024)S(1)} %pad_clamp_fusion), kind=kCustom, calls=%fused_computation.5 | custom fusion | bytes 10486016 | tf_op jit(solution)/shard_map/gather | solution.py:374
  435.1 0.6 gather_fusion.6
  435.7 0.1 sub.27
  435.8 0.0 copy-done
  435.8 5.4 %bitcast_divide_fusion = f32[5120,256]{1,0:T(8,128)} fusion(f32[64,80,256]{2,1,0:T(8,128)} %gather_fusion.5, f32[256]{0:T(256)S(1)} %copy-done, f32[5120]{0:T(1024)S(1)} %sub.27), kind=kLoop, calls=%fused_computation.8 | loop fusion | flops 2621440 | bytes 10507264 | tf_op jit(solution)/shard_map/div | solution.py:374
  (13 shorter events, 0.1 us)
Async XLA Ops:
  20.1 1.7 slice-start
  20.1 2.5 slice-start.1
  20.1 3.3 slice-start.2
  20.1 4.1 slice-start.3
  28.1 181.5 %all-to-all-start = ((f32[64,248,128]{2,1,0:T(8,128)}), f32[64,248,128]{2,1,0:T(8,128)}, u32[]{:S(2)}, u32[]{:S(2)}) async-start(f32[64,248,128]{2,1,0:T(8,128)} %pad_maximum_fusion), calls=%async_computation | async-start | bytes 16252928 | tf_op jit(solution)/shard_map/all_to_all | solution.py:360
  215.6 4.4 slice-start.4
  429.3 6.4 %copy-start = (f32[256]{0:T(256)S(1)}, f32[256]{0:T(256)}, u32[]{:S(2)}) copy-start(f32[256]{0:T(256)} %param.9) | copy-start | bytes 3076

commit v2 on v0

v2 whole, which is shorter than its diff:
```python
import functools

import jax
import jax.numpy as jnp
from jax import lax
from jax.experimental import pallas as pl
from jax.experimental.pallas import tpu as pltpu
from jax.sharding import PartitionSpec as P

MESH = pl.DeviceIdType.MESH
STEPS = 12
N_OCC = 4
DIGITS = ((1, 2), (2, 4), (8, 2), (16, 4))


def remote(src, dst, sems, k, peer):
    send, recv = sems
    return pltpu.make_async_remote_copy(
        src_ref=src, dst_ref=dst, send_sem=send.at[k], recv_sem=recv.at[k], device_id=peer, device_id_type=MESH
    )


def gcd16(n):
    g = 16
    while n % g:
        g //= 2
    return g


def panel_kernel(digits, per_step, owner_ref, amp_ref, out_ref, *scratch):
    levels = len(digits)
    arrived, kept, sems = scratch[:levels], scratch[levels : 2 * levels - 1], scratch[2 * levels - 1 :]
    occ, vir = lax.axis_index("occ"), lax.axis_index("vir")
    mine = [(vir // stride) % size for stride, size in digits]

    def along(level, digit):
        stride, _ = digits[level]
        return (occ, vir + (digit - mine[level]) * stride)

    peers = []
    for level, (_, size) in enumerate(digits):
        peers += [along(level, lax.rem(mine[level] + d, size)) for d in range(1, size)]
    barrier = pltpu.get_barrier_semaphore()
    for peer in peers:
        pl.semaphore_signal(barrier, inc=1, device_id=peer, device_id_type=MESH)
    pl.semaphore_wait(barrier, len(peers))

    k = 0
    started = []
    current, base, bases, lengths = amp_ref, 0, [], []
    length = amp_ref.shape[0]
    for level, (stride, size) in enumerate(digits):
        part = length // size
        copies = []
        for d in range(1, size):
            digit = lax.rem(mine[level] + d, size)
            copies.append(
                remote(current.at[pl.ds(digit * part, part)], arrived[level].at[d - 1], sems, k, along(level, digit))
            )
            k += 1
        for copy in copies:
            copy.start()
        offset = mine[level] * part
        base = base + offset
        target, target_base = (kept[level], 0) if level < levels - 1 else (out_ref, base)
        for copy in copies:
            copy.wait_recv()
        group = min(gcd16(part), per_step)
        for g in range(part // group):
            holder = owner_ref[(base + g * group) // per_step]
            digit = (holder // stride) % size
            value = current[pl.ds(offset + g * group, group)]
            for d in range(1, size):
                source = lax.rem(mine[level] + size - d, size)
                value = jnp.where(digit == source, arrived[level][d - 1, pl.ds(g * group, group)], value)
            target[pl.ds(target_base + g * group, group)] = value
        started += copies
        current, length = (target, part)
        bases.append(base)
        lengths.append(part)

    for level in range(levels - 1, -1, -1):
        piece = out_ref.at[pl.ds(bases[level], lengths[level])]
        copies = []
        for d in range(1, digits[level][1]):
            digit = lax.rem(mine[level] + d, digits[level][1])
            copies.append(remote(piece, piece, sems, k, along(level, digit)))
            k += 1
        for copy in copies:
            copy.start()
        for copy in copies:
            copy.wait_recv()
        started += copies

    for copy in started:
        copy.wait_send()


def broadcast_panels(amplitudes, panel_owner, digits):
    rows, cols = amplitudes.shape
    units = (rows // 8) * (cols // 128)
    amps = amplitudes.reshape(rows // 8, 8, cols // 128, 128).transpose(0, 2, 1, 3).reshape(units, 8, 128)
    per_step = units // STEPS
    arrived, kept, length, count = [], [], units, 0
    for level, (_, size) in enumerate(digits):
        length //= size
        arrived.append(pltpu.VMEM((size - 1, length, 8, 128), jnp.float32))
        kept.append(pltpu.VMEM((length, 8, 128), jnp.float32))
        count += (size - 1) * 2
    out = pl.pallas_call(
        functools.partial(panel_kernel, digits, per_step),
        out_shape=jax.ShapeDtypeStruct((units, 8, 128), jnp.float32),
        in_specs=[pl.BlockSpec(memory_space=pltpu.SMEM), pl.BlockSpec(memory_space=pltpu.VMEM)],
        out_specs=pl.BlockSpec(memory_space=pltpu.VMEM),
        scratch_shapes=arrived
        + kept[:-1]
        + [
            pltpu.SemaphoreType.DMA((count,)),
            pltpu.SemaphoreType.DMA((count,)),
        ],
        compiler_params=pltpu.CompilerParams(collective_id=0, has_side_effects=True),
        name="panels",
    )(panel_owner, amps)
    return out.reshape(rows // 8, cols // 128, 8, 128).transpose(0, 2, 1, 3).reshape(rows, cols)


CHUNKS = 5
LANES = 128


def chunk_rows(block):
    size = 3 * (block // CHUNKS)
    sizes = [size + 8] + [size] * (CHUNKS - 1)
    return [sum(sizes[:c]) for c in range(CHUNKS)], sizes


def pack_kernel(first_ref, second_ref, ints_ref, eps_ref, out_ref, turned):
    depth, col_count = ints_ref.shape
    blocks = eps_ref.shape[0]
    block = col_count // blocks
    group = 8
    fine = block // CHUNKS
    offsets, _ = chunk_rows(block)

    @pl.when(pl.program_id(0) == 0)
    def _():
        for n in range(blocks // group):
            at = slice(n * group * block, (n + 1) * group * block)
            turned[at, 0:depth] = ints_ref[:, at].T

    low_lane = lax.broadcasted_iota(jnp.int32, (block, LANES), 1) < LANES // 2
    for i in range(out_ref.shape[0]):
        dest = pl.program_id(0) * out_ref.shape[0] + i
        one, two = first_ref[dest], second_ref[dest]
        row_one, row_two = pl.multiple_of(one * block, 8), pl.multiple_of(two * block, 8)
        main_one, main_two = turned[pl.ds(row_one, block), 0:LANES], turned[pl.ds(row_two, block), 0:LANES]
        fold = jnp.where(
            low_lane,
            turned[pl.ds(row_one, block), LANES : 2 * LANES],
            pltpu.roll(turned[pl.ds(row_two, block), LANES : 2 * LANES], LANES // 2, 1),
        )
        for c, offset in enumerate(offsets):
            part = slice(c * fine, (c + 1) * fine)
            out_ref[i, offset : offset + fine] = main_one[part]
            out_ref[i, offset + fine : offset + 2 * fine] = main_two[part]
            out_ref[i, offset + 2 * fine : offset + 3 * fine] = fold[part]
        spare = offsets[0] + 3 * fine
        out_ref[i, spare : spare + 1] = eps_ref[pl.ds(one, 1)]
        out_ref[i, spare + 1 : spare + 2] = eps_ref[pl.ds(two, 1)]
        out_ref[i, spare + 2 : spare + 8] = jnp.zeros((6, LANES), jnp.float32)


def pack(integrals, energies, first, second):
    dests = first.shape[0]
    depth, col_count = integrals.shape
    blocks = energies.shape[0]
    rows = 3 * (col_count // blocks) + 8
    step = 8
    return pl.pallas_call(
        pack_kernel,
        out_shape=jax.ShapeDtypeStruct((dests, rows, LANES), jnp.float32),
        grid_spec=pltpu.PrefetchScalarGridSpec(
            num_scalar_prefetch=2,
            grid=(dests // step,),
            in_specs=[
                pl.BlockSpec((depth, col_count), lambda i, *_: (0, 0)),
                pl.BlockSpec((blocks, LANES), lambda i, *_: (0, 0)),
            ],
            out_specs=pl.BlockSpec((step, rows, LANES), lambda i, *_: (i, 0, 0)),
            scratch_shapes=[pltpu.VMEM((col_count, 2 * LANES), jnp.float32)],
        ),
        name="pack",
    )(first, second, integrals, energies)


def place_kernel(source_ref, ladder_ref, eps_ref, occ_ref, out_ref):
    chunks, _, two_fine, _ = ladder_ref.shape
    fine = two_fine // 2
    block = chunks * fine
    for i in range(out_ref.shape[0] // block):
        source = source_ref[pl.program_id(0) * (out_ref.shape[0] // block) + i]
        pair, half = source // 2, source % 2
        columns = eps_ref[pair].T
        column = jnp.where(half == 0, columns[:, 0:1], columns[:, 1:2])
        for c in range(chunks):
            value = ladder_ref[c, pair, pl.ds(pl.multiple_of(half * fine, 8), fine)]
            out_ref[pl.ds(i * block + c * fine, fine)] = value / (column[c * fine : (c + 1) * fine] - occ_ref[...])


def place(ladder, eps, eps_occ, source):
    chunks, pairs, two_fine, width = ladder.shape
    block = chunks * two_fine // 2
    blocks = source.shape[0]
    step = 8
    return pl.pallas_call(
        place_kernel,
        out_shape=jax.ShapeDtypeStruct((blocks * block, width), jnp.float32),
        grid_spec=pltpu.PrefetchScalarGridSpec(
            num_scalar_prefetch=1,
            grid=(blocks // step,),
            in_specs=[
                pl.BlockSpec(ladder.shape, lambda i, *_: (0, 0, 0, 0)),
                pl.BlockSpec(eps.shape, lambda i, *_: (0, 0, 0)),
                pl.BlockSpec((1, width), lambda i, *_: (0, 0)),
            ],
            out_specs=pl.BlockSpec((step * block, width), lambda i, *_: (i, 0)),
        ),
        name="place",
    )(source, ladder, eps, eps_occ[None, :])


def ladder_kernel(geometry, slot_ref, packed_ref, panel_ref, out_ref, eps_ref, *scratch):
    inner, senders = geometry
    near, scratch = scratch[:CHUNKS], scratch[CHUNKS:]
    (away, compact, held, passing, result, passing_result, panels, passing_panels, high, low, left_high, left_low,
     xy_send, xy_recv, own_sem, flip_send, flip_recv, send, recv, panel_send, panel_recv) = scratch
    pairs, slabs = compact.shape[1], near[0].shape[0] // 2
    share = pairs // N_OCC
    part = share // 2
    rows = compact.shape[2]
    fine = rows // 3
    width = panel_ref.shape[1]
    depth = panel_ref.shape[0] // N_OCC
    offsets, sizes = chunk_rows(fine * CHUNKS)

    occ, vir = lax.axis_index("occ"), lax.axis_index("vir")
    level = (vir // inner) % 2
    plane = (vir // (2 * inner)) * inner + vir % inner
    above, below, far = (lax.rem(occ + n, N_OCC) for n in (1, N_OCC - 1, 2))
    up, down = (above, vir), (below, vir)
    other = vir + inner * (1 - 2 * level)
    inside = (occ, other)
    turn = 2 * level - 1
    across = (lax.rem(occ + N_OCC + turn, N_OCC), other)
    core = vir % 2
    sibling = (occ, vir + 1 - 2 * core)

    def member(q):
        return (occ, (q // inner) * (2 * inner) + level * inner + q % inner)

    barrier = pltpu.get_barrier_semaphore()

    def greet(n, _):
        pl.semaphore_signal(barrier, inc=1, device_id=member(lax.rem(plane + n, slabs)), device_id_type=MESH)
        return 0

    lax.fori_loop(1, slabs, greet, 0)
    for peer in (up, down, inside, across):
        pl.semaphore_signal(barrier, inc=1, device_id=peer, device_id_type=MESH)
    pl.semaphore_wait(barrier, slabs - 1 + 4)

    def make(src, dst, sems, at, peer):
        return pltpu.make_async_remote_copy(
            src_ref=src, dst_ref=dst, send_sem=sems[0].at[at], recv_sem=sems[1].at[at], device_id=peer,
            device_id_type=MESH,
        )

    def span(c):
        return pl.ds(offsets[c], sizes[c])

    def away_of(c):
        return away.at[c] if c == 0 else away.at[c, :, pl.ds(0, sizes[c])]

    half = panel_ref.shape[0] // 2
    quarter = half // 2
    start = pl.multiple_of(core * half, 8)

    def panel_rows(which, offset, size):
        return panels.at[which, pl.ds(start + offset, size)]

    panel_sems = (panel_send, panel_recv)
    own_rows = lambda offset, size: panel_ref.at[pl.ds(start + offset, size)]
    panel_copies = [
        make(own_rows(0, quarter), passing_panels.at[0], panel_sems, 0, up),
        make(own_rows(quarter, quarter), passing_panels.at[1], panel_sems, 1, down),
        make(own_rows(0, half), panel_rows(occ, 0, half), panel_sems, 2, up),
        make(own_rows(0, half), panel_rows(occ, 0, half), panel_sems, 3, down),
        make(passing_panels.at[0], panel_rows(below, 0, quarter), panel_sems, 4, up),
        make(passing_panels.at[1], panel_rows(above, quarter, quarter), panel_sems, 5, down),
        make(panel_rows(below, 0, half), panel_rows(below, 0, half), panel_sems, 6, sibling),
        make(panel_rows(above, 0, half), panel_rows(above, 0, half), panel_sems, 7, sibling),
        make(panel_rows(far, 0, half), panel_rows(far, 0, half), panel_sems, 8, sibling),
    ]
    own_panel = pltpu.make_async_copy(panel_ref, panels.at[occ], own_sem.at[0])
    own_panel.start()
    for k in range(4):
        panel_copies[k].start()

    def scatter(c):
        def one(n, _):
            q = lax.rem(plane + n, slabs)
            make(packed_ref.at[level, q, span(c)], near[c].at[plane], (xy_send, xy_recv), 2 * c, member(q)).start()
            make(packed_ref.at[1 - level, q, span(c)], away_of(c).at[plane], (xy_send, xy_recv), 2 * c + 1,
                 member(q)).start()
            return 0

        lax.fori_loop(1, slabs, one, 0)
        own_of(c, 0).start()
        own_of(c, 1).start()

    def own_of(c, which):
        if which == 0:
            return pltpu.make_async_copy(packed_ref.at[level, plane, span(c)], near[c].at[plane], own_sem.at[1 + 2 * c])
        return pltpu.make_async_copy(
            packed_ref.at[1 - level, plane, span(c)], away_of(c).at[plane], own_sem.at[2 + 2 * c]
        )

    def whole(ref, count, sem):
        at = ref.at[pl.ds(0, count)]
        return pltpu.make_async_copy(at, at, sem)

    def flips(c):
        count = slabs // 2
        source = away_of(c)
        return [
            make(source.at[pl.ds(n * count, count)], near[c].at[pl.ds(slabs + n * count, count)],
                 (flip_send, flip_recv), 2 * c + n, peer)
            for n, peer in enumerate((inside, across))
        ]

    def exchange(c, kind):
        sems, at = (send, recv), 12 * c + kind
        mine = pl.ds(occ * share, share)
        to = lambda which, offset=0, size=share: pl.ds(which * share + offset, size)
        if kind == 0:
            return make(compact.at[c, to(far, 0, part)], passing.at[c, 0], sems, at, up)
        if kind == 1:
            return make(compact.at[c, to(far, part, part)], passing.at[c, 1], sems, at, down)
        if kind == 2:
            return make(compact.at[c, to(above)], held.at[c, occ], sems, at, up)
        if kind == 3:
            return make(compact.at[c, to(below)], held.at[c, occ], sems, at, down)
        if kind == 4:
            return make(passing.at[c, 0], held.at[c, below, pl.ds(0, part)], sems, at, up)
        if kind == 5:
            return make(passing.at[c, 1], held.at[c, above, pl.ds(part, part)], sems, at, down)
        if kind == 6:
            return make(result.at[c, far, pl.ds(0, part)], passing_result.at[c, 0], sems, at, up)
        if kind == 7:
            return make(result.at[c, far, pl.ds(part, part)], passing_result.at[c, 1], sems, at, down)
        if kind == 8:
            return make(result.at[c, above], out_ref.at[c, mine], sems, at, up)
        if kind == 9:
            return make(result.at[c, below], out_ref.at[c, mine], sems, at, down)
        if kind == 10:
            return make(passing_result.at[c, 0], out_ref.at[c, to(below, 0, part)], sems, at, up)
        return make(passing_result.at[c, 1], out_ref.at[c, to(above, part, part)], sems, at, down)

    def gather(c):
        whole(away_of(c), slabs - 1, xy_recv.at[2 * c + 1]).wait()
        own_of(c, 1).wait()
        for copy in flips(c):
            copy.start()
        whole(near[c], slabs - 1, xy_recv.at[2 * c]).wait()
        own_of(c, 0).wait()

    def select(c):
        for copy in flips(c):
            copy.wait_recv()

        def one(p, _):
            slab = near[c][slot_ref[p]]
            compact[c, p] = slab[:rows]
            if c == 0:
                eps_ref[p] = slab[rows : rows + 8]
            return 0

        lax.fori_loop(0, pairs, one, 0)
        for kind in range(4):
            exchange(c, kind).start()
        local = pl.ds(occ * share, share)

        def keep(p, _):
            held[c, occ, p] = compact[c, occ * share + p]
            return 0

        lax.fori_loop(0, share, keep, 0)

    def relay(c):
        for n in range(2):
            exchange(c, n).wait_recv()
            exchange(c, 4 + n).start()

    def prepare():
        own_panel.wait()
        for n in range(N_OCC):
            pieces = ((n * depth, n * LANES, LANES), (n * depth + LANES, N_OCC * LANES + n * (depth - LANES), depth - LANES))
            for origin, target, count in pieces:
                for o in range(N_OCC):
                    value = panels[o, origin : origin + count]
                    upper = value.astype(jnp.bfloat16)
                    high[target : target + count, o * width : (o + 1) * width] = upper
                    low[target : target + count, o * width : (o + 1) * width] = (
                        value - upper.astype(jnp.float32)
                    ).astype(jnp.bfloat16)

    def compute(c):
        for kind in range(2, 6):
            exchange(c, kind).wait_recv()
        low_lane = lax.broadcasted_iota(jnp.int32, (fine, LANES), 1) < LANES // 2

        def arrange(p, _):
            turned = slot_ref[occ * share + p] >= slabs + slabs // 2
            value = [
                jnp.where(turned, held[c, lax.rem(n + N_OCC - turn, N_OCC), p], held[c, n, p]) for n in range(N_OCC)
            ]
            tiles = [v[: 2 * fine] for v in value]
            folds = [v[2 * fine :] for v in value]
            for n in range(0, N_OCC, 2):
                one = jnp.where(low_lane, folds[n], pltpu.roll(folds[n + 1], LANES // 2, 1))
                two = jnp.where(low_lane, pltpu.roll(folds[n], LANES // 2, 1), folds[n + 1])
                tiles.append(jnp.concatenate([one, two], axis=0))
            full = jnp.concatenate(tiles, axis=1)
            upper = full.astype(jnp.bfloat16)
            at = pl.ds(pl.multiple_of(p * 2 * fine, 16), 2 * fine)
            left_high[at] = upper
            left_low[at] = (full - upper.astype(jnp.float32)).astype(jnp.bfloat16)
            return 0

        lax.fori_loop(0, share, arrange, 0)
        for o in range(N_OCC):
            at = slice(o * width, (o + 1) * width)
            dot = lambda a, b: jnp.dot(a[...], b[:, at], preferred_element_type=jnp.float32)
            total = (dot(left_high, low) + dot(left_low, high)) + dot(left_high, high)
            result[c, o] = total.reshape(share, 2 * fine, width)
        out_ref[c, pl.ds(occ * share, share)] = result[c, occ]
        for kind in range(6, 10):
            exchange(c, kind).start()

    def relay_result(c):
        for n in range(2):
            exchange(c, 6 + n).wait_recv()
            exchange(c, 10 + n).start()

    scatter(0)
    scatter(1)
    for n in range(2):
        panel_copies[n].wait_recv()
        panel_copies[4 + n].start()
    for s in range(CHUNKS + 4):
        if 2 <= s + 2 < CHUNKS:
            scatter(s + 2)
        if s < CHUNKS:
            gather(s)
        if 0 <= s - 1 < CHUNKS:
            select(s - 1)
        if s == 1:
            for n in range(2):
                panel_copies[2 + n].wait_recv()
                panel_copies[6 + n].start()
            for n in range(2):
                panel_copies[4 + n].wait_recv()
            panel_copies[8].start()
        if 0 <= s - 2 < CHUNKS:
            relay(s - 2)
        if s == 2:
            for n in range(3):
                panel_copies[6 + n].wait_recv()
            prepare()
        if 0 <= s - 3 < CHUNKS:
            compute(s - 3)
        if 0 <= s - 4 < CHUNKS:
            relay_result(s - 4)

    for c in range(CHUNKS):
        for kind in range(8, 12):
            exchange(c, kind).wait_recv()
        for kind in range(12):
            exchange(c, kind).wait_send()
        for copy in flips(c):
            copy.wait_send()
        whole(near[c], slabs - 1, xy_send.at[2 * c]).wait()
        whole(away_of(c), slabs - 1, xy_send.at[2 * c + 1]).wait()
    for copy in panel_copies:
        copy.wait_send()


def ladder_of(packed, panel, slot_of, inner):
    _, slabs, total_rows, lanes = packed.shape
    pairs = slot_of.shape[0]
    depth, width = panel.shape
    share = pairs // N_OCC
    _, sizes = chunk_rows((total_rows - 8) // 3)
    rows = sizes[-1]
    fine = rows // 3
    f32, bf16 = jnp.float32, jnp.bfloat16
    vmem, dma = pl.BlockSpec(memory_space=pltpu.VMEM), pltpu.SemaphoreType.DMA
    return pl.pallas_call(
        functools.partial(ladder_kernel, (inner, 2 * slabs)),
        out_shape=[
            jax.ShapeDtypeStruct((CHUNKS, pairs, 2 * fine, width), f32),
            jax.ShapeDtypeStruct((pairs, 8, lanes), f32),
        ],
        in_specs=[pl.BlockSpec(memory_space=pltpu.SMEM), pl.BlockSpec(memory_space=pl.ANY), vmem],
        out_specs=[vmem, vmem],
        scratch_shapes=[pltpu.VMEM((2 * slabs, size, lanes), f32) for size in sizes]
        + [
            pltpu.VMEM((CHUNKS, slabs, sizes[0], lanes), f32),
            pltpu.VMEM((CHUNKS, pairs, rows, lanes), f32),
            pltpu.VMEM((CHUNKS, N_OCC, share, rows, lanes), f32),
            pltpu.VMEM((CHUNKS, 2, share // 2, rows, lanes), f32),
            pltpu.VMEM((CHUNKS, N_OCC, share, 2 * fine, width), f32),
            pltpu.VMEM((CHUNKS, 2, share // 2, 2 * fine, width), f32),
            pltpu.VMEM((N_OCC, depth, width), f32),
            pltpu.VMEM((2, depth // 4, width), f32),
            pltpu.VMEM((depth, N_OCC * width), bf16),
            pltpu.VMEM((depth, N_OCC * width), bf16),
            pltpu.VMEM((share * 2 * fine, depth), bf16),
            pltpu.VMEM((share * 2 * fine, depth), bf16),
            dma((2 * CHUNKS,)),
            dma((2 * CHUNKS,)),
            dma((1 + 2 * CHUNKS,)),
            dma((2 * CHUNKS,)),
            dma((2 * CHUNKS,)),
            dma((12 * CHUNKS,)),
            dma((12 * CHUNKS,)),
            dma((9,)),
            dma((9,)),
        ],
        compiler_params=pltpu.CompilerParams(collective_id=1, has_side_effects=True, vmem_limit_bytes=60 * 2**20),
        name="ladder",
    )(slot_of, packed, panel)


def local(amplitudes, integrals, eps_vir, eps_occ, panel_owner, block_target):
    me = lax.axis_index("vir")
    senders = lax.axis_size("vir")
    depth, col_count = integrals.shape
    blocks_dev = block_target.shape[0] // senders
    block = col_count // blocks_dev
    stride, levels = DIGITS[2]
    inner = stride
    slabs = senders // levels

    owners = block_target.reshape(senders, blocks_dev) // blocks_dev
    position = jnp.arange(blocks_dev, dtype=jnp.int32)
    order = jnp.arange(senders, dtype=jnp.int32)
    dest = order % slabs
    dest = (dest // inner) * (levels * inner) + (order // slabs) * inner + dest % inner
    goes = lax.dynamic_index_in_dim(owners, me, 0, keepdims=False)[None, :] == dest[:, None]
    first = jnp.min(jnp.where(goes, position[None, :], blocks_dev - 1), axis=1)
    second = jnp.max(jnp.where(goes, position[None, :], 0), axis=1)

    comes = owners == me
    sends = jnp.any(comes, axis=1)
    level = (order // inner) % levels
    slot = (order // (levels * inner)) * inner + order % inner
    slot = slot + jnp.where(level == (me // inner) % levels, 0, slabs)
    rank = jnp.sum((sends[None, :] & (slot[None, :] < slot[:, None])).astype(jnp.int32), axis=1)
    pair = jnp.arange(senders // 2, dtype=jnp.int32)
    slot_of = jnp.sum(jnp.where(sends[None, :] & (rank[None, :] == pair[:, None]), slot[None, :], 0), axis=1)
    lead = jnp.min(jnp.where(comes, position[None, :], blocks_dev), axis=1)
    stands = 2 * rank[:, None] + (position[None, :] != lead[:, None]).astype(jnp.int32)
    wanted = me * blocks_dev + position
    found = block_target.reshape(1, senders, blocks_dev) == wanted[:, None, None]
    source = jnp.sum(jnp.where(found, stands[None], 0), axis=(1, 2))

    energies = jnp.pad(eps_vir.reshape(blocks_dev, block), ((0, 0), (0, LANES - block)))
    packed = pack(integrals, energies, first, second)
    packed = packed.reshape(levels, slabs, packed.shape[1], LANES)
    panel = broadcast_panels(amplitudes, panel_owner, DIGITS)
    ladder, eps = ladder_of(packed, panel, slot_of, inner)
    return place(ladder, eps, eps_occ, source)


def solution(mesh):
    in_specs = (P("vir", "occ"), P("occ", "vir"), P("vir"), P("occ"), P(), P())
    out_specs = P("vir", "occ")
    return jax.shard_map(local, mesh=mesh, in_specs=in_specs, out_specs=out_specs, check_vma=False)
```

time: 1020 us -> 356 us (0.35)
  waiting for transfers between devices: 920 us -> 0 us
  Pallas kernels: 0 us -> 350 us
  local copies, waits for them, and re-layouts: 45 us -> 2.22 us
  between operations: 22.4 us -> 0.04 us
  matrix products: 18.8 us -> 0 us
    psum x1 -> x0, waiting for transfers between devices: 784 us -> none  [broadcast(): return lax.psum(block, axis)]
    pallas_call x0 -> x4, Pallas kernels: none -> 350 us  [the longest x1 295 us: ladder_of(): pl.pallas_call(functools.partial(ladder_kernel, (inner, 2 * slabs)), out_...]
    all_to_all x1 -> x0, waiting for transfers between devices: 135 us -> none  [local(): lax.all_to_all(buffer, 'vir', split_axis=0, concat_axis=0, tiled=True)]
    dot_general x1 -> x0, matrix products: 18.8 us -> none  [local(): lax.dot_general(lax.all_gather(integrals, 'occ', axis=0, tiled=True), pan...]
    scatter x1 -> x0, local copies, waits for them, and re-layouts: 13.8 us -> none  [pack(): return buffer.at[owner_list, rank_list].set(blocks)]
  transfers between devices with their start and end apart: 3 -> 0, of which waited for: 2 -> 0; matrix products, arithmetic and copies ran while one was open for 1% -> 0% of each run, Pallas kernels for 0% -> 0%
where the time goes in v2:
time: 356 us
  Pallas kernels  350 us (98%)
  other arithmetic  3.77 us (1%)
    pallas_call x1, Pallas kernels, ladder_of(): pl.pallas_call(functools.partial(ladder_kernel, (inner, 2 * slabs)), out_...  295 us
    pallas_call x1, Pallas kernels, broadcast_panels(): pl.pallas_call(functools.partial(panel_kernel, digits, per_step), out_sha...  35.9 us
    pallas_call x1, Pallas kernels, place(): pl.pallas_call(place_kernel, out_shape=jax.ShapeDtypeStruct((blocks * blo...  9.57 us
    pallas_call x1, Pallas kernels, pack(): pl.pallas_call(pack_kernel, out_shape=jax.ShapeDtypeStruct((dests, rows,...  9.11 us

profile of v2, /device:TPU:1, one launch (start us, length us, event | category | flops | bytes accessed | tf_op | source)
XLA Modules:
  0.0 355.6 jit_solution(5785948083964453708)
XLA Ops:
  0.0 0.8 eq.70
  0.8 0.8 reshape.199
  1.6 0.6 pad.4.eps_ref
  2.2 0.1 fusion.13
  2.4 0.2 select_reduce_fusion.1
  2.6 0.7 select_reduce_fusion.2.slot_ref
  3.3 0.8 fusion.1
  4.0 0.1 convert_add_fusion
  4.1 1.9 select_reduce_fusion.source_ref
  6.0 35.9 %panels.1 = f32[192,8,128]{2,1,0:T(8,128)} custom-call(s32[12]{0:T(128)} %owner_ref.1, f32[192,8,128]{2,1,0:T(8,128)} %bitcast.16), custom_call_target="tpu_custom_call" | custom-call | tf_op jit(solution)/shard_map/panels/pallas_call | solution.py:110
  41.9 9.1 %pack.1 = f32[64,248,128]{2,1,0:T(8,128)} custom-call(s32[64]{0:T(128)} %get-tuple-element.10.first_ref, s32[64]{0:T(128)} %get-tuple-element.9.second_ref, f32[192,5120]{1,0:T(8,128)} %ints_ref.1, f32[64,128]{1,0:T(8,128)} %pad.4.eps_ref), custom_call_target="tpu_custom_call" | custom-call | tf_op jit(solution)/shard_map/pack/pallas_call | solution.py:179
  51.0 295.0 %ladder.1 = (f32[5,32,32,256]{3,2,1,0:T(8,128)}, f32[32,8,128]{2,1,0:T(8,128)}) custom-call(s32[32]{0:T(128)} %select_reduce_fusion.2.slot_ref, f32[2,32,248,128]{3,2,1,0:T(8,128)} %bitcast.14, f32[768,256]{1,0:T(8,128)} %bitcast.15), custom_call_target="tpu_custom_call" | custom-call | tf_op jit(solution)/shard_map/ladder/pallas_call | solution.py:508
  346.1 9.6 %place.1 = f32[5120,256]{1,0:T(8,128)} custom-call(s32[64]{0:T(128)} %select_reduce_fusion.source_ref, f32[5,32,32,256]{3,2,1,0:T(8,128)} %get-tuple-element.7.ladder_ref, f32[32,8,128]{2,1,0:T(8,128)} %get-tuple-element.8.eps_ref, f32[1,256]{1,0:T(1,128)} %bitcast.17), custom_call_target="tpu_custom_call" | custom-call | tf_op jit(solution)/shard_map/place/pallas_call | solution.py:215
  (5 shorter events, 0.0 us)

commit v3 on v2

--- a/solution.py
+++ b/solution.py
@@ -10,14 +10,7 @@
 MESH = pl.DeviceIdType.MESH
 STEPS = 12
 N_OCC = 4
-DIGITS = ((1, 2), (2, 4), (8, 2), (16, 4))
-
-
-def remote(src, dst, sems, k, peer):
-    send, recv = sems
-    return pltpu.make_async_remote_copy(
-        src_ref=src, dst_ref=dst, send_sem=send.at[k], recv_sem=recv.at[k], device_id=peer, device_id_type=MESH
-    )
+DIGITS = ((1, 2), (8, 2), (2, 4), (16, 4))
 
 
 def gcd16(n):
@@ -25,103 +18,6 @@
     while n % g:
         g //= 2
     return g
-
-
-def panel_kernel(digits, per_step, owner_ref, amp_ref, out_ref, *scratch):
-    levels = len(digits)
-    arrived, kept, sems = scratch[:levels], scratch[levels : 2 * levels - 1], scratch[2 * levels - 1 :]
-    occ, vir = lax.axis_index("occ"), lax.axis_index("vir")
-    mine = [(vir // stride) % size for stride, size in digits]
-
-    def along(level, digit):
-        stride, _ = digits[level]
-        return (occ, vir + (digit - mine[level]) * stride)
-
-    peers = []
-    for level, (_, size) in enumerate(digits):
-        peers += [along(level, lax.rem(mine[level] + d, size)) for d in range(1, size)]
-    barrier = pltpu.get_barrier_semaphore()
-    for peer in peers:
-        pl.semaphore_signal(barrier, inc=1, device_id=peer, device_id_type=MESH)
-    pl.semaphore_wait(barrier, len(peers))
-
-    k = 0
-    started = []
-    current, base, bases, lengths = amp_ref, 0, [], []
-    length = amp_ref.shape[0]
-    for level, (stride, size) in enumerate(digits):
-        part = length // size
-        copies = []
-        for d in range(1, size):
-            digit = lax.rem(mine[level] + d, size)
-            copies.append(
-                remote(current.at[pl.ds(digit * part, part)], arrived[level].at[d - 1], sems, k, along(level, digit))
-            )
-            k += 1
-        for copy in copies:
-            copy.start()
-        offset = mine[level] * part
-        base = base + offset
-        target, target_base = (kept[level], 0) if level < levels - 1 else (out_ref, base)
-        for copy in copies:
-            copy.wait_recv()
-        group = min(gcd16(part), per_step)
-        for g in range(part // group):
-            holder = owner_ref[(base + g * group) // per_step]
-            digit = (holder // stride) % size
-            value = current[pl.ds(offset + g * group, group)]
-            for d in range(1, size):
-                source = lax.rem(mine[level] + size - d, size)
-                value = jnp.where(digit == source, arrived[level][d - 1, pl.ds(g * group, group)], value)
-            target[pl.ds(target_base + g * group, group)] = value
-        started += copies
-        current, length = (target, part)
-        bases.append(base)
-        lengths.append(part)
-
-    for level in range(levels - 1, -1, -1):
-        piece = out_ref.at[pl.ds(bases[level], lengths[level])]
-        copies = []
-        for d in range(1, digits[level][1]):
-            digit = lax.rem(mine[level] + d, digits[level][1])
-            copies.append(remote(piece, piece, sems, k, along(level, digit)))
-            k += 1
-        for copy in copies:
-            copy.start()
-        for copy in copies:
-            copy.wait_recv()
-        started += copies
-
-    for copy in started:
-        copy.wait_send()
-
-
-def broadcast_panels(amplitudes, panel_owner, digits):
-    rows, cols = amplitudes.shape
-    units = (rows // 8) * (cols // 128)
-    amps = amplitudes.reshape(rows // 8, 8, cols // 128, 128).transpose(0, 2, 1, 3).reshape(units, 8, 128)
-    per_step = units // STEPS
-    arrived, kept, length, count = [], [], units, 0
-    for level, (_, size) in enumerate(digits):
-        length //= size
-        arrived.append(pltpu.VMEM((size - 1, length, 8, 128), jnp.float32))
-        kept.append(pltpu.VMEM((length, 8, 128), jnp.float32))
-        count += (size - 1) * 2
-    out = pl.pallas_call(
-        functools.partial(panel_kernel, digits, per_step),
-        out_shape=jax.ShapeDtypeStruct((units, 8, 128), jnp.float32),
-        in_specs=[pl.BlockSpec(memory_space=pltpu.SMEM), pl.BlockSpec(memory_space=pltpu.VMEM)],
-        out_specs=pl.BlockSpec(memory_space=pltpu.VMEM),
-        scratch_shapes=arrived
-        + kept[:-1]
-        + [
-            pltpu.SemaphoreType.DMA((count,)),
-            pltpu.SemaphoreType.DMA((count,)),
-        ],
-        compiler_params=pltpu.CompilerParams(collective_id=0, has_side_effects=True),
-        name="panels",
-    )(panel_owner, amps)
-    return out.reshape(rows // 8, cols // 128, 8, 128).transpose(0, 2, 1, 3).reshape(rows, cols)
 
 
 CHUNKS = 5
@@ -193,21 +89,18 @@
     )(first, second, integrals, energies)
 
 
-def place_kernel(source_ref, ladder_ref, eps_ref, occ_ref, out_ref):
+def place_kernel(source_ref, ladder_ref, out_ref):
     chunks, _, two_fine, _ = ladder_ref.shape
     fine = two_fine // 2
     block = chunks * fine
     for i in range(out_ref.shape[0] // block):
         source = source_ref[pl.program_id(0) * (out_ref.shape[0] // block) + i]
         pair, half = source // 2, source % 2
-        columns = eps_ref[pair].T
-        column = jnp.where(half == 0, columns[:, 0:1], columns[:, 1:2])
         for c in range(chunks):
-            value = ladder_ref[c, pair, pl.ds(pl.multiple_of(half * fine, 8), fine)]
-            out_ref[pl.ds(i * block + c * fine, fine)] = value / (column[c * fine : (c + 1) * fine] - occ_ref[...])
-
-
-def place(ladder, eps, eps_occ, source):
+            out_ref[pl.ds(i * block + c * fine, fine)] = ladder_ref[c, pair, pl.ds(pl.multiple_of(half * fine, 8), fine)]
+
+
+def place(ladder, source):
     chunks, pairs, two_fine, width = ladder.shape
     block = chunks * two_fine // 2
     blocks = source.shape[0]
@@ -218,29 +111,29 @@
         grid_spec=pltpu.PrefetchScalarGridSpec(
             num_scalar_prefetch=1,
             grid=(blocks // step,),
-            in_specs=[
-                pl.BlockSpec(ladder.shape, lambda i, *_: (0, 0, 0, 0)),
-                pl.BlockSpec(eps.shape, lambda i, *_: (0, 0, 0)),
-                pl.BlockSpec((1, width), lambda i, *_: (0, 0)),
-            ],
+            in_specs=[pl.BlockSpec(ladder.shape, lambda i, *_: (0, 0, 0, 0))],
             out_specs=pl.BlockSpec((step * block, width), lambda i, *_: (i, 0)),
         ),
         name="place",
-    )(source, ladder, eps, eps_occ[None, :])
-
-
-def ladder_kernel(geometry, slot_ref, packed_ref, panel_ref, out_ref, eps_ref, *scratch):
-    inner, senders = geometry
+    )(source, ladder)
+
+
+def ladder_kernel(digits, slot_ref, owner_ref, packed_ref, amp_ref, eocc_ref, out_ref, *scratch):
+    inner = digits[1][0]
+    levels = len(digits)
     near, scratch = scratch[:CHUNKS], scratch[CHUNKS:]
-    (away, compact, held, passing, result, passing_result, panels, passing_panels, high, low, left_high, left_low,
-     xy_send, xy_recv, own_sem, flip_send, flip_recv, send, recv, panel_send, panel_recv) = scratch
+    arrived, kept, scratch = scratch[:levels], scratch[levels : 2 * levels - 1], scratch[2 * levels - 1 :]
+    (away, compact, held, passing, result, passing_result, panels, high, low, left_high, left_low, eps_ref, eps_col,
+     energies, xy_send, xy_recv, own_sem, flip_send, flip_recv, send, recv, panel_send, panel_recv) = scratch
     pairs, slabs = compact.shape[1], near[0].shape[0] // 2
     share = pairs // N_OCC
     part = share // 2
     rows = compact.shape[2]
     fine = rows // 3
-    width = panel_ref.shape[1]
-    depth = panel_ref.shape[0] // N_OCC
+    width = out_ref.shape[3]
+    units = amp_ref.shape[0]
+    per_step, across_units = units // STEPS, width // LANES
+    depth = (units // across_units) * 8 // N_OCC
     offsets, sizes = chunk_rows(fine * CHUNKS)
 
     occ, vir = lax.axis_index("occ"), lax.axis_index("vir")
@@ -258,6 +151,11 @@
     def member(q):
         return (occ, (q // inner) * (2 * inner) + level * inner + q % inner)
 
+    mine_digit = [(vir // stride) % size for stride, size in digits]
+
+    def along(n, digit):
+        return (occ, vir + (digit - mine_digit[n]) * digits[n][0])
+
     barrier = pltpu.get_barrier_semaphore()
 
     def greet(n, _):
@@ -281,30 +179,78 @@
     def away_of(c):
         return away.at[c] if c == 0 else away.at[c, :, pl.ds(0, sizes[c])]
 
-    half = panel_ref.shape[0] // 2
-    quarter = half // 2
-    start = pl.multiple_of(core * half, 8)
-
-    def panel_rows(which, offset, size):
-        return panels.at[which, pl.ds(start + offset, size)]
-
     panel_sems = (panel_send, panel_recv)
-    own_rows = lambda offset, size: panel_ref.at[pl.ds(start + offset, size)]
-    panel_copies = [
-        make(own_rows(0, quarter), passing_panels.at[0], panel_sems, 0, up),
-        make(own_rows(quarter, quarter), passing_panels.at[1], panel_sems, 1, down),
-        make(own_rows(0, half), panel_rows(occ, 0, half), panel_sems, 2, up),
-        make(own_rows(0, half), panel_rows(occ, 0, half), panel_sems, 3, down),
-        make(passing_panels.at[0], panel_rows(below, 0, quarter), panel_sems, 4, up),
-        make(passing_panels.at[1], panel_rows(above, quarter, quarter), panel_sems, 5, down),
-        make(panel_rows(below, 0, half), panel_rows(below, 0, half), panel_sems, 6, sibling),
-        make(panel_rows(above, 0, half), panel_rows(above, 0, half), panel_sems, 7, sibling),
-        make(panel_rows(far, 0, half), panel_rows(far, 0, half), panel_sems, 8, sibling),
+    panel_copies = []
+
+    def panel_start(pieces):
+        copies = [make(src, dst, panel_sems, len(panel_copies) + n, peer) for n, (src, dst, peer) in enumerate(pieces)]
+        panel_copies.extend(copies)
+        for copy in copies:
+            copy.start()
+        return copies
+
+    def panel_stages():
+        current, base, length, bases, lengths = amp_ref, 0, units, [], []
+        for n, (stride, size) in enumerate(digits):
+            part = length // size
+            pieces = []
+            for d in range(1, size):
+                digit = lax.rem(mine_digit[n] + d, size)
+                pieces.append((current.at[pl.ds(digit * part, part)], arrived[n].at[d - 1], along(n, digit)))
+            copies = panel_start(pieces)
+            yield
+            offset = mine_digit[n] * part
+            base = base + offset
+            target, target_base = (kept[n], 0) if n < levels - 1 else (panels.at[occ], base)
+            for copy in copies:
+                copy.wait_recv()
+            group = min(gcd16(part), per_step)
+            for g in range(part // group):
+                holder = owner_ref[(base + g * group) // per_step]
+                digit = (holder // stride) % size
+                value = current[pl.ds(offset + g * group, group)]
+                for d in range(1, size):
+                    source = lax.rem(mine_digit[n] + size - d, size)
+                    value = jnp.where(digit == source, arrived[n][d - 1, pl.ds(g * group, group)], value)
+                target[pl.ds(target_base + g * group, group)] = value
+            current, length = target, part
+            bases.append(base)
+            lengths.append(part)
+        for n in range(levels - 1, 1, -1):
+            piece = panels.at[occ, pl.ds(bases[n], lengths[n])]
+            copies = panel_start(
+                [(piece, piece, along(n, lax.rem(mine_digit[n] + d, digits[n][1]))) for d in range(1, digits[n][1])]
+            )
+            yield
+            for copy in copies:
+                copy.wait_recv()
+        around = 2 * N_OCC
+        z = 2 * occ + level
+        z_up, z_down = (lax.rem(occ + level, N_OCC), other), (lax.rem(occ + N_OCC - 1 + level, N_OCC), other)
+        quarter, half = lengths[1], lengths[0]
+        core = vir % 2
+        for n in range(1, around // 2 + 1):
+            pieces = []
+            for sign, peer in ((-1, z_up), (1, z_down))[: 2 if n < around // 2 else 1]:
+                origin = lax.rem(z + around + sign * (n - 1), around)
+                piece = panels.at[origin // 2, pl.ds(core * half + (origin % 2) * quarter, quarter)]
+                pieces.append((piece, piece, peer))
+            copies = panel_start(pieces)
+            yield
+            for copy in copies:
+                copy.wait_recv()
+        piece = panels.at[:, pl.ds(core * half, half)]
+        copies = panel_start([(piece, piece, along(0, 1 - mine_digit[0]))])
+        yield
+        copies[0].wait_recv()
+        prepare()
+        yield
+
+    energy_copies = [
+        make(eocc_ref, energies.at[occ], (send, recv), 12 * CHUNKS, up),
+        make(eocc_ref, energies.at[occ], (send, recv), 12 * CHUNKS + 1, down),
+        make(energies.at[below], energies.at[below], (send, recv), 12 * CHUNKS + 2, up),
     ]
-    own_panel = pltpu.make_async_copy(panel_ref, panels.at[occ], own_sem.at[0])
-    own_panel.start()
-    for k in range(4):
-        panel_copies[k].start()
 
     def scatter(c):
         def one(n, _):
@@ -402,17 +348,18 @@
             exchange(c, 4 + n).start()
 
     def prepare():
-        own_panel.wait()
         for n in range(N_OCC):
             pieces = ((n * depth, n * LANES, LANES), (n * depth + LANES, N_OCC * LANES + n * (depth - LANES), depth - LANES))
             for origin, target, count in pieces:
                 for o in range(N_OCC):
-                    value = panels[o, origin : origin + count]
-                    upper = value.astype(jnp.bfloat16)
-                    high[target : target + count, o * width : (o + 1) * width] = upper
-                    low[target : target + count, o * width : (o + 1) * width] = (
-                        value - upper.astype(jnp.float32)
-                    ).astype(jnp.bfloat16)
+                    stacked = panels[o, origin // 8 * across_units : (origin + count) // 8 * across_units]
+                    stacked = stacked.reshape(count // 8, across_units, 8, LANES)
+                    for k in range(across_units):
+                        value = stacked[:, k].reshape(count, LANES)
+                        upper = value.astype(jnp.bfloat16)
+                        at = slice(o * width + k * LANES, o * width + (k + 1) * LANES)
+                        high[target : target + count, at] = upper
+                        low[target : target + count, at] = (value - upper.astype(jnp.float32)).astype(jnp.bfloat16)
 
     def compute(c):
         for kind in range(2, 6):
@@ -435,6 +382,8 @@
             at = pl.ds(pl.multiple_of(p * 2 * fine, 16), 2 * fine)
             left_high[at] = upper
             left_low[at] = (full - upper.astype(jnp.float32)).astype(jnp.bfloat16)
+            columns = eps_ref[occ * share + p].T[c * fine : (c + 1) * fine]
+            eps_col[at] = jnp.concatenate([columns[:, 0:1], columns[:, 1:2]], axis=0)
             return 0
 
         lax.fori_loop(0, share, arrange, 0)
@@ -442,6 +391,7 @@
             at = slice(o * width, (o + 1) * width)
             dot = lambda a, b: jnp.dot(a[...], b[:, at], preferred_element_type=jnp.float32)
             total = (dot(left_high, low) + dot(left_low, high)) + dot(left_high, high)
+            total = total / (eps_col[...] - energies[o, 0:1])
             result[c, o] = total.reshape(share, 2 * fine, width)
         out_ref[c, pl.ds(occ * share, share)] = result[c, occ]
         for kind in range(6, 10):
@@ -452,31 +402,39 @@
             exchange(c, 6 + n).wait_recv()
             exchange(c, 10 + n).start()
 
+    panel = panel_stages()
+    next(panel, None)
+    for n in range(2):
+        energy_copies[n].start()
+    energies[occ] = eocc_ref[...]
     scatter(0)
-    scatter(1)
-    for n in range(2):
-        panel_copies[n].wait_recv()
-        panel_copies[4 + n].start()
+    for _ in range(3):
+        next(panel, None)
     for s in range(CHUNKS + 4):
-        if 2 <= s + 2 < CHUNKS:
-            scatter(s + 2)
         if s < CHUNKS:
             gather(s)
+        if s == 0:
+            next(panel, None)
+            next(panel, None)
+        if 1 <= s + 1 < CHUNKS:
+            scatter(s + 1)
         if 0 <= s - 1 < CHUNKS:
             select(s - 1)
         if s == 1:
+            next(panel, None)
             for n in range(2):
-                panel_copies[2 + n].wait_recv()
-                panel_copies[6 + n].start()
-            for n in range(2):
-                panel_copies[4 + n].wait_recv()
-            panel_copies[8].start()
+                energy_copies[n].wait_recv()
+            energy_copies[2].start()
+        if s == 2:
+            next(panel, None)
         if 0 <= s - 2 < CHUNKS:
             relay(s - 2)
         if s == 2:
-            for n in range(3):
-                panel_copies[6 + n].wait_recv()
-            prepare()
+            next(panel, None)
+        if s == 3:
+            for _ in range(3):
+                next(panel, None)
+            energy_copies[2].wait_recv()
         if 0 <= s - 3 < CHUNKS:
             compute(s - 3)
         if 0 <= s - 4 < CHUNKS:
@@ -491,29 +449,37 @@
             copy.wait_send()
         whole(near[c], slabs - 1, xy_send.at[2 * c]).wait()
         whole(away_of(c), slabs - 1, xy_send.at[2 * c + 1]).wait()
-    for copy in panel_copies:
+    for copy in panel_copies + energy_copies:
         copy.wait_send()
 
 
-def ladder_of(packed, panel, slot_of, inner):
+def ladder_of(packed, amplitudes, eps_occ, panel_owner, slot_of, digits):
     _, slabs, total_rows, lanes = packed.shape
     pairs = slot_of.shape[0]
-    depth, width = panel.shape
+    panel_rows, width = amplitudes.shape
     share = pairs // N_OCC
     _, sizes = chunk_rows((total_rows - 8) // 3)
     rows = sizes[-1]
     fine = rows // 3
     f32, bf16 = jnp.float32, jnp.bfloat16
     vmem, dma = pl.BlockSpec(memory_space=pltpu.VMEM), pltpu.SemaphoreType.DMA
+    smem = pl.BlockSpec(memory_space=pltpu.SMEM)
+    units = (panel_rows // 8) * (width // lanes)
+    amps = amplitudes.reshape(panel_rows // 8, 8, width // lanes, lanes).transpose(0, 2, 1, 3).reshape(units, 8, lanes)
+    arrived, kept, length, count = [], [], units, 2 * N_OCC
+    for n, (_, size) in enumerate(digits):
+        length //= size
+        arrived.append(pltpu.VMEM((size - 1, length, 8, lanes), f32))
+        kept.append(pltpu.VMEM((length, 8, lanes), f32))
+        count += (size - 1) * (2 if n > 1 else 1)
     return pl.pallas_call(
-        functools.partial(ladder_kernel, (inner, 2 * slabs)),
-        out_shape=[
-            jax.ShapeDtypeStruct((CHUNKS, pairs, 2 * fine, width), f32),
-            jax.ShapeDtypeStruct((pairs, 8, lanes), f32),
-        ],
-        in_specs=[pl.BlockSpec(memory_space=pltpu.SMEM), pl.BlockSpec(memory_space=pl.ANY), vmem],
-        out_specs=[vmem, vmem],
+        functools.partial(ladder_kernel, digits),
+        out_shape=jax.ShapeDtypeStruct((CHUNKS, pairs, 2 * fine, width), f32),
+        in_specs=[smem, smem, pl.BlockSpec(memory_space=pl.ANY), vmem, vmem],
+        out_specs=vmem,
         scratch_shapes=[pltpu.VMEM((2 * slabs, size, lanes), f32) for size in sizes]
+        + arrived
+        + kept[:-1]
         + [
             pltpu.VMEM((CHUNKS, slabs, sizes[0], lanes), f32),
             pltpu.VMEM((CHUNKS, pairs, rows, lanes), f32),
@@ -521,25 +487,27 @@
             pltpu.VMEM((CHUNKS, 2, share // 2, rows, lanes), f32),
             pltpu.VMEM((CHUNKS, N_OCC, share, 2 * fine, width), f32),
             pltpu.VMEM((CHUNKS, 2, share // 2, 2 * fine, width), f32),
-            pltpu.VMEM((N_OCC, depth, width), f32),
-            pltpu.VMEM((2, depth // 4, width), f32),
-            pltpu.VMEM((depth, N_OCC * width), bf16),
-            pltpu.VMEM((depth, N_OCC * width), bf16),
-            pltpu.VMEM((share * 2 * fine, depth), bf16),
-            pltpu.VMEM((share * 2 * fine, depth), bf16),
+            pltpu.VMEM((N_OCC, units, 8, lanes), f32),
+            pltpu.VMEM((panel_rows, N_OCC * width), bf16),
+            pltpu.VMEM((panel_rows, N_OCC * width), bf16),
+            pltpu.VMEM((share * 2 * fine, panel_rows), bf16),
+            pltpu.VMEM((share * 2 * fine, panel_rows), bf16),
+            pltpu.VMEM((pairs, 8, lanes), f32),
+            pltpu.VMEM((share * 2 * fine, 1), f32),
+            pltpu.VMEM((N_OCC, 8, width), f32),
             dma((2 * CHUNKS,)),
             dma((2 * CHUNKS,)),
             dma((1 + 2 * CHUNKS,)),
             dma((2 * CHUNKS,)),
             dma((2 * CHUNKS,)),
-            dma((12 * CHUNKS,)),
-            dma((12 * CHUNKS,)),
-            dma((9,)),
-            dma((9,)),
+            dma((12 * CHUNKS + 3,)),
+            dma((12 * CHUNKS + 3,)),
+            dma((count,)),
+            dma((count,)),
         ],
         compiler_params=pltpu.CompilerParams(collective_id=1, has_side_effects=True, vmem_limit_bytes=60 * 2**20),
         name="ladder",
-    )(slot_of, packed, panel)
+    )(slot_of, panel_owner, packed, amps, jnp.broadcast_to(eps_occ[None, :], (8, width)))
 
 
 def local(amplitudes, integrals, eps_vir, eps_occ, panel_owner, block_target):
@@ -548,7 +516,7 @@
     depth, col_count = integrals.shape
     blocks_dev = block_target.shape[0] // senders
     block = col_count // blocks_dev
-    stride, levels = DIGITS[2]
+    stride, levels = DIGITS[1]
     inner = stride
     slabs = senders // levels
 
@@ -578,9 +546,8 @@
     energies = jnp.pad(eps_vir.reshape(blocks_dev, block), ((0, 0), (0, LANES - block)))
     packed = pack(integrals, energies, first, second)
     packed = packed.reshape(levels, slabs, packed.shape[1], LANES)
-    panel = broadcast_panels(amplitudes, panel_owner, DIGITS)
-    ladder, eps = ladder_of(packed, panel, slot_of, inner)
-    return place(ladder, eps, eps_occ, source)
+    ladder = ladder_of(packed, amplitudes, eps_occ, panel_owner, slot_of, DIGITS)
+    return place(ladder, source)
 
 
 def solution(mesh):

time: 356 us -> 369 us (1.037)
  the two profiles are of different devices: /device:TPU:1 before, /device:TPU:13 now
where the time goes in v3:
time: 369 us
  Pallas kernels  361 us (98%)
  other arithmetic  3.73 us (1%)
    pallas_call x1, Pallas kernels, ladder_of(): pl.pallas_call(functools.partial(ladder_kernel, digits), out_shape=jax.Sh...  345 us
    pallas_call x1, Pallas kernels, pack(): pl.pallas_call(pack_kernel, out_shape=jax.ShapeDtypeStruct((dests, rows,...  9.1 us

profile of v3, /device:TPU:13, one launch (start us, length us, event | category | flops | bytes accessed | tf_op | source)
XLA Modules:
  0.0 368.7 jit_solution(11269037049522321996)
XLA Ops:
  0.0 1.3 broadcast_in_dim.74.eocc_ref
  1.3 0.8 eq.70
  2.1 0.8 reshape.194
  2.9 0.6 pad.4.eps_ref
  3.5 0.1 fusion.13
  3.6 0.2 select_reduce_fusion.1
  3.8 0.6 select_reduce_fusion.2.slot_ref
  4.5 0.8 fusion.1
  5.2 0.1 convert_add_fusion
  5.3 1.9 select_reduce_fusion.source_ref
  7.2 9.1 %pack.1 = f32[64,248,128]{2,1,0:T(8,128)} custom-call(s32[64]{0:T(128)} %get-tuple-element.6.first_ref, s32[64]{0:T(128)} %get-tuple-element.5.second_ref, f32[192,5120]{1,0:T(8,128)} %ints_ref.1, f32[64,128]{1,0:T(8,128)} %pad.4.eps_ref), custom_call_target="tpu_custom_call" | custom-call | tf_op jit(solution)/shard_map/pack/pallas_call | solution.py:75
  16.3 345.4 %ladder.1.ladder_ref = f32[5,32,32,256]{3,2,1,0:T(8,128)} custom-call(s32[32]{0:T(128)} %select_reduce_fusion.2.slot_ref, s32[12]{0:T(128)} %owner_ref.1, f32[2,32,248,128]{3,2,1,0:T(8,128)} %bitcast.8, f32[192,8,128]{2,1,0:T(8,128)} %bitcast.9, f32[8,256]{1,0:T(8,128)} %broadcast_in_dim.74.eocc_ref), custom_call_target="tpu_custom_call" | custom-call | tf_op jit(solution)/shard_map/ladder/pallas_call | solution.py:475
  361.8 6.9 %place.1 = f32[5120,256]{1,0:T(8,128)} custom-call(s32[64]{0:T(128)} %select_reduce_fusion.source_ref, f32[5,32,32,256]{3,2,1,0:T(8,128)} %ladder.1.ladder_ref), custom_call_target="tpu_custom_call" | custom-call | tf_op jit(solution)/shard_map/place/pallas_call | solution.py:108
  (5 shorter events, 0.0 us)

commit v4 on v3

--- a/solution.py
+++ b/solution.py
@@ -20,8 +20,15 @@
     return g
 
 
-CHUNKS = 5
+CHUNKS = 10
 LANES = 128
+ORDER = (
+    "A0", "P", "P", "A1", "B0", "P", "A2", "S0", "B1", "D0", "P", "A3", "S1", "R0", "P", "B2", "D1", "B3", "P",
+    "R1", "S2", "S3", "A4", "A5", "P", "D2", "P", "B4", "R2", "P", "A6", "A7", "S4", "B5", "P", "D3", "A8",
+    "S5", "R3", "B6", "R4", "B7", "P", "P", "B8", "D4", "R5", "S6", "C0", "S7", "A9", "Q0", "C1", "C2", "D5",
+    "D6", "C3", "Q1", "S8", "B9", "D7", "Q2", "R6", "C4", "S9", "C5", "Q3", "R7", "R8", "D8", "R9", "Q4", "C6",
+    "D9", "C7", "C8", "Q5", "C9", "Q6", "Q7", "Q8", "Q9",
+)
 
 
 def chunk_rows(block):
@@ -332,9 +339,12 @@
             return 0
 
         lax.fori_loop(0, pairs, one, 0)
-        for kind in range(4):
+        for kind in range(2):
             exchange(c, kind).start()
-        local = pl.ds(occ * share, share)
+
+    def direct(c):
+        for kind in range(2, 4):
+            exchange(c, kind).start()
 
         def keep(p, _):
             held[c, occ, p] = compact[c, occ * share + p]
@@ -402,43 +412,22 @@
             exchange(c, 6 + n).wait_recv()
             exchange(c, 10 + n).start()
 
-    panel = panel_stages()
-    next(panel, None)
     for n in range(2):
         energy_copies[n].start()
     energies[occ] = eocc_ref[...]
-    scatter(0)
-    for _ in range(3):
-        next(panel, None)
-    for s in range(CHUNKS + 4):
-        if s < CHUNKS:
-            gather(s)
-        if s == 0:
+    panel = panel_stages()
+    steps = {"A": scatter, "B": gather, "S": select, "D": direct, "R": relay, "C": compute, "Q": relay_result}
+    for name in ORDER:
+        if name == "P":
             next(panel, None)
-            next(panel, None)
-        if 1 <= s + 1 < CHUNKS:
-            scatter(s + 1)
-        if 0 <= s - 1 < CHUNKS:
-            select(s - 1)
-        if s == 1:
-            next(panel, None)
+            continue
+        if name == "R0":
             for n in range(2):
                 energy_copies[n].wait_recv()
             energy_copies[2].start()
-        if s == 2:
-            next(panel, None)
-        if 0 <= s - 2 < CHUNKS:
-            relay(s - 2)
-        if s == 2:
-            next(panel, None)
-        if s == 3:
-            for _ in range(3):
-                next(panel, None)
+        if name == "C0":
             energy_copies[2].wait_recv()
-        if 0 <= s - 3 < CHUNKS:
-            compute(s - 3)
-        if 0 <= s - 4 < CHUNKS:
-            relay_result(s - 4)
+        steps[name[0]](int(name[1:]))
 
     for c in range(CHUNKS):
         for kind in range(8, 12):

time: 369 us -> 320 us (0.87)
  the two profiles are of different devices: /device:TPU:13 before, /device:TPU:1 now
where the time goes in v4:
time: 320 us
  Pallas kernels  313 us (98%)
  other arithmetic  3.73 us (1%)
  local copies, waits for them, and re-layouts  3.49 us (1%)
    pallas_call x1, Pallas kernels, ladder_of(): pl.pallas_call(functools.partial(ladder_kernel, digits), out_shape=jax.Sh...  297 us
    pallas_call x1, Pallas kernels, pack(): pl.pallas_call(pack_kernel, out_shape=jax.ShapeDtypeStruct((dests, rows,...  9.1 us
    pallas_call x1, Pallas kernels, place(): pl.pallas_call(place_kernel, out_shape=jax.ShapeDtypeStruct((blocks * blo...  6.93 us

profile of v4, /device:TPU:1, one launch (start us, length us, event | category | flops | bytes accessed | tf_op | source)
XLA Modules:
  0.0 319.9 jit_solution(17244958039427050401)
XLA Ops:
  0.0 1.3 broadcast_in_dim.74.eocc_ref
  1.3 0.8 eq.70
  2.1 0.8 reshape.194
  2.9 0.6 pad.4.eps_ref
  3.5 0.1 fusion.13
  3.6 0.2 select_reduce_fusion.1
  3.8 0.6 select_reduce_fusion.2.slot_ref
  4.5 0.8 fusion.1
  5.2 0.1 convert_add_fusion
  5.3 1.9 select_reduce_fusion.source_ref
  7.2 9.1 %pack.1 = f32[64,248,128]{2,1,0:T(8,128)} custom-call(s32[64]{0:T(128)} %get-tuple-element.6.first_ref, s32[64]{0:T(128)} %get-tuple-element.5.second_ref, f32[192,5120]{1,0:T(8,128)} %ints_ref.1, f32[64,128]{1,0:T(8,128)} %pad.4.eps_ref), custom_call_target="tpu_custom_call" | custom-call | tf_op jit(solution)/shard_map/pack/pallas_call | solution.py:82
  16.3 296.7 %ladder.1.ladder_ref = f32[10,32,16,256]{3,2,1,0:T(8,128)} custom-call(s32[32]{0:T(128)} %select_reduce_fusion.2.slot_ref, s32[12]{0:T(128)} %owner_ref.1, f32[2,32,248,128]{3,2,1,0:T(8,128)} %bitcast.8, f32[192,8,128]{2,1,0:T(8,128)} %bitcast.9, f32[8,256]{1,0:T(8,128)} %broadcast_in_dim.74.eocc_ref), custom_call_target="tpu_custom_call" | custom-call | tf_op jit(solution)/shard_map/ladder/pallas_call | solution.py:464
  313.0 6.9 %place.1 = f32[5120,256]{1,0:T(8,128)} custom-call(s32[64]{0:T(128)} %select_reduce_fusion.source_ref, f32[10,32,16,256]{3,2,1,0:T(8,128)} %ladder.1.ladder_ref), custom_call_target="tpu_custom_call" | custom-call | tf_op jit(solution)/shard_map/place/pallas_call | solution.py:115
  (5 shorter events, 0.0 us)

commit v5 on v4

--- a/solution.py
+++ b/solution.py
@@ -23,12 +23,14 @@
 CHUNKS = 10
 LANES = 128
 ORDER = (
-    "A0", "P", "P", "A1", "B0", "P", "A2", "S0", "B1", "D0", "P", "A3", "S1", "R0", "P", "B2", "D1", "B3", "P",
-    "R1", "S2", "S3", "A4", "A5", "P", "D2", "P", "B4", "R2", "P", "A6", "A7", "S4", "B5", "P", "D3", "A8",
-    "S5", "R3", "B6", "R4", "B7", "P", "P", "B8", "D4", "R5", "S6", "C0", "S7", "A9", "Q0", "C1", "C2", "D5",
-    "D6", "C3", "Q1", "S8", "B9", "D7", "Q2", "R6", "C4", "S9", "C5", "Q3", "R7", "R8", "D8", "R9", "Q4", "C6",
-    "D9", "C7", "C8", "Q5", "C9", "Q6", "Q7", "Q8", "Q9",
+    "A0", "A1", "P", "B0", "A2", "P", "S0", "P", "B1", "R0", "B2", "P", "S1", "D0", "P", "P", "D1", "A3", "S2",
+    "R1", "A4", "P", "A5", "B3", "B4", "A6", "S3", "S4", "P", "B5", "A7", "B6", "D2", "S5", "A8", "P", "S6",
+    "B7", "R2", "R3", "P", "B8", "S7", "P", "D3", "R4", "P", "D4", "R5", "A9", "C0", "C1", "C2", "S8", "R6",
+    "B9", "D5", "D6", "D7", "C3", "S9", "C4", "R7", "C5", "D8", "R8", "R9", "C6", "D9", "C7", "C8", "C9",
 )
+
+
+KINDS = 8
 
 
 def chunk_rows(block):
@@ -130,11 +132,10 @@
     levels = len(digits)
     near, scratch = scratch[:CHUNKS], scratch[CHUNKS:]
     arrived, kept, scratch = scratch[:levels], scratch[levels : 2 * levels - 1], scratch[2 * levels - 1 :]
-    (away, compact, held, passing, result, passing_result, panels, high, low, left_high, left_low, eps_ref, eps_col,
+    (away, compact, held, result, panels, high, low, left_high, left_low, eps_ref, eps_col,
      energies, xy_send, xy_recv, own_sem, flip_send, flip_recv, send, recv, panel_send, panel_recv) = scratch
     pairs, slabs = compact.shape[1], near[0].shape[0] // 2
     share = pairs // N_OCC
-    part = share // 2
     rows = compact.shape[2]
     fine = rows // 3
     width = out_ref.shape[3]
@@ -254,9 +255,9 @@
         yield
 
     energy_copies = [
-        make(eocc_ref, energies.at[occ], (send, recv), 12 * CHUNKS, up),
-        make(eocc_ref, energies.at[occ], (send, recv), 12 * CHUNKS + 1, down),
-        make(energies.at[below], energies.at[below], (send, recv), 12 * CHUNKS + 2, up),
+        make(eocc_ref, energies.at[occ], (send, recv), KINDS * CHUNKS, up),
+        make(eocc_ref, energies.at[occ], (send, recv), KINDS * CHUNKS + 1, down),
+        make(energies.at[below], energies.at[below], (send, recv), KINDS * CHUNKS + 2, up),
     ]
 
     def scatter(c):
@@ -292,32 +293,23 @@
         ]
 
     def exchange(c, kind):
-        sems, at = (send, recv), 12 * c + kind
-        mine = pl.ds(occ * share, share)
-        to = lambda which, offset=0, size=share: pl.ds(which * share + offset, size)
+        sems, at = (send, recv), KINDS * c + kind
+        group = lambda shift: pl.ds(lax.rem(occ + N_OCC + shift, N_OCC) * share, share)
         if kind == 0:
-            return make(compact.at[c, to(far, 0, part)], passing.at[c, 0], sems, at, up)
+            return make(compact.at[c, group(0)], held.at[c, 0, occ], sems, at, up)
         if kind == 1:
-            return make(compact.at[c, to(far, part, part)], passing.at[c, 1], sems, at, down)
+            return make(compact.at[c, group(1)], held.at[c, 1, occ], sems, at, down)
         if kind == 2:
-            return make(compact.at[c, to(above)], held.at[c, occ], sems, at, up)
+            return make(compact.at[c, group(-1)], held.at[c, 1, occ], sems, at, up)
         if kind == 3:
-            return make(compact.at[c, to(below)], held.at[c, occ], sems, at, down)
+            return make(compact.at[c, group(-2)], held.at[c, 0, occ], sems, at, down)
         if kind == 4:
-            return make(passing.at[c, 0], held.at[c, below, pl.ds(0, part)], sems, at, up)
+            return make(held.at[c, 0, below], held.at[c, 1, below], sems, at, up)
         if kind == 5:
-            return make(passing.at[c, 1], held.at[c, above, pl.ds(part, part)], sems, at, down)
+            return make(held.at[c, 1, above], held.at[c, 0, above], sems, at, down)
         if kind == 6:
-            return make(result.at[c, far, pl.ds(0, part)], passing_result.at[c, 0], sems, at, up)
-        if kind == 7:
-            return make(result.at[c, far, pl.ds(part, part)], passing_result.at[c, 1], sems, at, down)
-        if kind == 8:
-            return make(result.at[c, above], out_ref.at[c, mine], sems, at, up)
-        if kind == 9:
-            return make(result.at[c, below], out_ref.at[c, mine], sems, at, down)
-        if kind == 10:
-            return make(passing_result.at[c, 0], out_ref.at[c, to(below, 0, part)], sems, at, up)
-        return make(passing_result.at[c, 1], out_ref.at[c, to(above, part, part)], sems, at, down)
+            return make(result.at[c, 0], out_ref.at[c, group(-1)], sems, at, down)
+        return make(result.at[c, 1], out_ref.at[c, group(-2)], sems, at, up)
 
     def gather(c):
         whole(away_of(c), slabs - 1, xy_recv.at[2 * c + 1]).wait()
@@ -347,7 +339,8 @@
             exchange(c, kind).start()
 
         def keep(p, _):
-            held[c, occ, p] = compact[c, occ * share + p]
+            for role in range(2):
+                held[c, role, occ, p] = compact[c, lax.rem(occ + N_OCC - 1 - role, N_OCC) * share + p]
             return 0
 
         lax.fori_loop(0, share, keep, 0)
@@ -367,19 +360,22 @@
                     for k in range(across_units):
                         value = stacked[:, k].reshape(count, LANES)
                         upper = value.astype(jnp.bfloat16)
-                        at = slice(o * width + k * LANES, o * width + (k + 1) * LANES)
-                        high[target : target + count, at] = upper
-                        low[target : target + count, at] = (value - upper.astype(jnp.float32)).astype(jnp.bfloat16)
+                        at = slice(k * LANES, (k + 1) * LANES)
+                        high[o, target : target + count, at] = upper
+                        low[o, target : target + count, at] = (value - upper.astype(jnp.float32)).astype(jnp.bfloat16)
 
     def compute(c):
         for kind in range(2, 6):
             exchange(c, kind).wait_recv()
         low_lane = lax.broadcasted_iota(jnp.int32, (fine, LANES), 1) < LANES // 2
 
-        def arrange(p, _):
-            turned = slot_ref[occ * share + p] >= slabs + slabs // 2
+        def arrange(q, _):
+            role, p = q // share, q % share
+            number = lax.rem(occ + N_OCC - 1 - role, N_OCC) * share + p
+            turned = slot_ref[number] >= slabs + slabs // 2
             value = [
-                jnp.where(turned, held[c, lax.rem(n + N_OCC - turn, N_OCC), p], held[c, n, p]) for n in range(N_OCC)
+                jnp.where(turned, held[c, role, lax.rem(n + N_OCC - turn, N_OCC), p], held[c, role, n, p])
+                for n in range(N_OCC)
             ]
             tiles = [v[: 2 * fine] for v in value]
             folds = [v[2 * fine :] for v in value]
@@ -389,34 +385,34 @@
                 tiles.append(jnp.concatenate([one, two], axis=0))
             full = jnp.concatenate(tiles, axis=1)
             upper = full.astype(jnp.bfloat16)
-            at = pl.ds(pl.multiple_of(p * 2 * fine, 16), 2 * fine)
+            at = pl.ds(pl.multiple_of(q * 2 * fine, 16), 2 * fine)
             left_high[at] = upper
             left_low[at] = (full - upper.astype(jnp.float32)).astype(jnp.bfloat16)
-            columns = eps_ref[occ * share + p].T[c * fine : (c + 1) * fine]
+            columns = eps_ref[number].T[c * fine : (c + 1) * fine]
             eps_col[at] = jnp.concatenate([columns[:, 0:1], columns[:, 1:2]], axis=0)
             return 0
 
-        lax.fori_loop(0, share, arrange, 0)
-        for o in range(N_OCC):
-            at = slice(o * width, (o + 1) * width)
-            dot = lambda a, b: jnp.dot(a[...], b[:, at], preferred_element_type=jnp.float32)
-            total = (dot(left_high, low) + dot(left_low, high)) + dot(left_high, high)
-            total = total / (eps_col[...] - energies[o, 0:1])
-            result[c, o] = total.reshape(share, 2 * fine, width)
-        out_ref[c, pl.ds(occ * share, share)] = result[c, occ]
-        for kind in range(6, 10):
+        lax.fori_loop(0, 2 * share, arrange, 0)
+        tall = share * 2 * fine
+        for role, other_one in enumerate((below, above)):
+            rows_of = pl.ds(role * tall, tall)
+            for o in (other_one, occ):
+                dot = lambda a, b: jnp.dot(a[rows_of], b[o], preferred_element_type=jnp.float32)
+                total = (dot(left_high, low) + dot(left_low, high)) + dot(left_high, high)
+                total = total / (eps_col[rows_of] - energies[o, 0:1])
+                total = total.reshape(share, 2 * fine, width)
+                if o is occ:
+                    out_ref[c, pl.ds(lax.rem(occ + N_OCC - 1 - role, N_OCC) * share, share)] = total
+                else:
+                    result[c, role] = total
+        for kind in range(6, 8):
             exchange(c, kind).start()
-
-    def relay_result(c):
-        for n in range(2):
-            exchange(c, 6 + n).wait_recv()
-            exchange(c, 10 + n).start()
 
     for n in range(2):
         energy_copies[n].start()
     energies[occ] = eocc_ref[...]
     panel = panel_stages()
-    steps = {"A": scatter, "B": gather, "S": select, "D": direct, "R": relay, "C": compute, "Q": relay_result}
+    steps = {"A": scatter, "B": gather, "S": select, "D": direct, "R": relay, "C": compute}
     for name in ORDER:
         if name == "P":
             next(panel, None)
@@ -430,9 +426,9 @@
         steps[name[0]](int(name[1:]))
 
     for c in range(CHUNKS):
-        for kind in range(8, 12):
+        for kind in range(6, 8):
             exchange(c, kind).wait_recv()
-        for kind in range(12):
+        for kind in range(KINDS):
             exchange(c, kind).wait_send()
         for copy in flips(c):
             copy.wait_send()
@@ -472,31 +468,29 @@
         + [
             pltpu.VMEM((CHUNKS, slabs, sizes[0], lanes), f32),
             pltpu.VMEM((CHUNKS, pairs, rows, lanes), f32),
-            pltpu.VMEM((CHUNKS, N_OCC, share, rows, lanes), f32),
-            pltpu.VMEM((CHUNKS, 2, share // 2, rows, lanes), f32),
-            pltpu.VMEM((CHUNKS, N_OCC, share, 2 * fine, width), f32),
-            pltpu.VMEM((CHUNKS, 2, share // 2, 2 * fine, width), f32),
+            pltpu.VMEM((CHUNKS, 2, N_OCC, share, rows, lanes), f32),
+            pltpu.VMEM((CHUNKS, 2, share, 2 * fine, width), f32),
             pltpu.VMEM((N_OCC, units, 8, lanes), f32),
-            pltpu.VMEM((panel_rows, N_OCC * width), bf16),
-            pltpu.VMEM((panel_rows, N_OCC * width), bf16),
-            pltpu.VMEM((share * 2 * fine, panel_rows), bf16),
-            pltpu.VMEM((share * 2 * fine, panel_rows), bf16),
+            pltpu.VMEM((N_OCC, panel_rows, width), bf16),
+            pltpu.VMEM((N_OCC, panel_rows, width), bf16),
+            pltpu.VMEM((share * 4 * fine, panel_rows), bf16),
+            pltpu.VMEM((share * 4 * fine, panel_rows), bf16),
             pltpu.VMEM((pairs, 8, lanes), f32),
-            pltpu.VMEM((share * 2 * fine, 1), f32),
-            pltpu.VMEM((N_OCC, 8, width), f32),
+            pltpu.VMEM((share * 4 * fine, 1), f32),
+            pltpu.VMEM((N_OCC, 1, width), f32),
             dma((2 * CHUNKS,)),
             dma((2 * CHUNKS,)),
             dma((1 + 2 * CHUNKS,)),
             dma((2 * CHUNKS,)),
             dma((2 * CHUNKS,)),
-            dma((12 * CHUNKS + 3,)),
-            dma((12 * CHUNKS + 3,)),
+            dma((KINDS * CHUNKS + 3,)),
+            dma((KINDS * CHUNKS + 3,)),
             dma((count,)),
             dma((count,)),
         ],
         compiler_params=pltpu.CompilerParams(collective_id=1, has_side_effects=True, vmem_limit_bytes=60 * 2**20),
         name="ladder",
-    )(slot_of, panel_owner, packed, amps, jnp.broadcast_to(eps_occ[None, :], (8, width)))
+    )(slot_of, panel_owner, packed, amps, eps_occ[None, :])
 
 
 def local(amplitudes, integrals, eps_vir, eps_occ, panel_owner, block_target):

time: 320 us -> 306 us (0.956)
  Pallas kernels: 313 us -> 300 us
    pallas_call x1, Pallas kernels: 297 us -> 284 us  [ladder_of(): pl.pallas_call(functools.partial(ladder_kernel, digits), out_shape=jax.Sh...]
where the time goes in v5:
time: 306 us
  Pallas kernels  300 us (98%)
  other arithmetic  3.73 us (1%)
    pallas_call x1, Pallas kernels, ladder_of(): pl.pallas_call(functools.partial(ladder_kernel, digits), out_shape=jax.Sh...  284 us
    pallas_call x1, Pallas kernels, pack(): pl.pallas_call(pack_kernel, out_shape=jax.ShapeDtypeStruct((dests, rows,...  9.1 us
    pallas_call x1, Pallas kernels, place(): pl.pallas_call(place_kernel, out_shape=jax.ShapeDtypeStruct((blocks * blo...  6.93 us

profile of v5, /device:TPU:1, one launch (start us, length us, event | category | flops | bytes accessed | tf_op | source)
XLA Modules:
  0.0 306.2 jit_solution(4625474492823226296)
XLA Ops:
  0.0 0.8 eq.70
  0.8 0.8 reshape.193
  1.6 0.6 pad.4.eps_ref
  2.2 0.1 fusion.13
  2.4 0.2 select_reduce_fusion.1
  2.6 0.7 select_reduce_fusion.2.slot_ref
  3.3 0.8 fusion.1
  4.0 0.1 convert_add_fusion
  4.1 1.9 select_reduce_fusion.source_ref
  6.0 9.1 %pack.1 = f32[64,248,128]{2,1,0:T(8,128)} custom-call(s32[64]{0:T(128)} %get-tuple-element.6.first_ref, s32[64]{0:T(128)} %get-tuple-element.5.second_ref, f32[192,5120]{1,0:T(8,128)} %ints_ref.1, f32[64,128]{1,0:T(8,128)} %pad.4.eps_ref), custom_call_target="tpu_custom_call" | custom-call | tf_op jit(solution)/shard_map/pack/pallas_call | solution.py:84
  15.1 284.2 %ladder.1.ladder_ref = f32[10,32,16,256]{3,2,1,0:T(8,128)} custom-call(s32[32]{0:T(128)} %select_reduce_fusion.2.slot_ref, s32[12]{0:T(128)} %owner_ref.1, f32[2,32,248,128]{3,2,1,0:T(8,128)} %bitcast.9, f32[192,8,128]{2,1,0:T(8,128)} %bitcast.10, f32[1,256]{1,0:T(1,128)} %bitcast.11), custom_call_target="tpu_custom_call" | custom-call | tf_op jit(solution)/shard_map/ladder/pallas_call | solution.py:460
  299.3 6.9 %place.1 = f32[5120,256]{1,0:T(8,128)} custom-call(s32[64]{0:T(128)} %select_reduce_fusion.source_ref, f32[10,32,16,256]{3,2,1,0:T(8,128)} %ladder.1.ladder_ref), custom_call_target="tpu_custom_call" | custom-call | tf_op jit(solution)/shard_map/place/pallas_call | solution.py:117
  (5 shorter events, 0.0 us)

commit v6 on v5

--- a/solution.py
+++ b/solution.py
@@ -35,67 +35,7 @@
 
 def chunk_rows(block):
     size = 3 * (block // CHUNKS)
-    sizes = [size + 8] + [size] * (CHUNKS - 1)
-    return [sum(sizes[:c]) for c in range(CHUNKS)], sizes
-
-
-def pack_kernel(first_ref, second_ref, ints_ref, eps_ref, out_ref, turned):
-    depth, col_count = ints_ref.shape
-    blocks = eps_ref.shape[0]
-    block = col_count // blocks
-    group = 8
-    fine = block // CHUNKS
-    offsets, _ = chunk_rows(block)
-
-    @pl.when(pl.program_id(0) == 0)
-    def _():
-        for n in range(blocks // group):
-            at = slice(n * group * block, (n + 1) * group * block)
-            turned[at, 0:depth] = ints_ref[:, at].T
-
-    low_lane = lax.broadcasted_iota(jnp.int32, (block, LANES), 1) < LANES // 2
-    for i in range(out_ref.shape[0]):
-        dest = pl.program_id(0) * out_ref.shape[0] + i
-        one, two = first_ref[dest], second_ref[dest]
-        row_one, row_two = pl.multiple_of(one * block, 8), pl.multiple_of(two * block, 8)
-        main_one, main_two = turned[pl.ds(row_one, block), 0:LANES], turned[pl.ds(row_two, block), 0:LANES]
-        fold = jnp.where(
-            low_lane,
-            turned[pl.ds(row_one, block), LANES : 2 * LANES],
-            pltpu.roll(turned[pl.ds(row_two, block), LANES : 2 * LANES], LANES // 2, 1),
-        )
-        for c, offset in enumerate(offsets):
-            part = slice(c * fine, (c + 1) * fine)
-            out_ref[i, offset : offset + fine] = main_one[part]
-            out_ref[i, offset + fine : offset + 2 * fine] = main_two[part]
-            out_ref[i, offset + 2 * fine : offset + 3 * fine] = fold[part]
-        spare = offsets[0] + 3 * fine
-        out_ref[i, spare : spare + 1] = eps_ref[pl.ds(one, 1)]
-        out_ref[i, spare + 1 : spare + 2] = eps_ref[pl.ds(two, 1)]
-        out_ref[i, spare + 2 : spare + 8] = jnp.zeros((6, LANES), jnp.float32)
-
-
-def pack(integrals, energies, first, second):
-    dests = first.shape[0]
-    depth, col_count = integrals.shape
-    blocks = energies.shape[0]
-    rows = 3 * (col_count // blocks) + 8
-    step = 8
-    return pl.pallas_call(
-        pack_kernel,
-        out_shape=jax.ShapeDtypeStruct((dests, rows, LANES), jnp.float32),
-        grid_spec=pltpu.PrefetchScalarGridSpec(
-            num_scalar_prefetch=2,
-            grid=(dests // step,),
-            in_specs=[
-                pl.BlockSpec((depth, col_count), lambda i, *_: (0, 0)),
-                pl.BlockSpec((blocks, LANES), lambda i, *_: (0, 0)),
-            ],
-            out_specs=pl.BlockSpec((step, rows, LANES), lambda i, *_: (i, 0, 0)),
-            scratch_shapes=[pltpu.VMEM((col_count, 2 * LANES), jnp.float32)],
-        ),
-        name="pack",
-    )(first, second, integrals, energies)
+    return [size + 8] + [size] * (CHUNKS - 1)
 
 
 def place_kernel(source_ref, ladder_ref, out_ref):
@@ -127,12 +67,16 @@
     )(source, ladder)
 
 
-def ladder_kernel(digits, slot_ref, owner_ref, packed_ref, amp_ref, eocc_ref, out_ref, *scratch):
+def ladder_kernel(
+    digits, slot_ref, owner_ref, first_ref, second_ref, ints_ref, evir_ref, amp_ref, eocc_ref, out_ref, *scratch
+):
     inner = digits[1][0]
     levels = len(digits)
-    near, scratch = scratch[:CHUNKS], scratch[CHUNKS:]
+    near, away, packed, scratch = (
+        scratch[:CHUNKS], scratch[CHUNKS : 2 * CHUNKS], scratch[2 * CHUNKS : 3 * CHUNKS], scratch[3 * CHUNKS :]
+    )
     arrived, kept, scratch = scratch[:levels], scratch[levels : 2 * levels - 1], scratch[2 * levels - 1 :]
-    (away, compact, held, result, panels, high, low, left_high, left_low, eps_ref, eps_col,
+    (turned, compact, held, result, panels, high, low, left_high, left_low, eps_ref, eps_col,
      energies, xy_send, xy_recv, own_sem, flip_send, flip_recv, send, recv, panel_send, panel_recv) = scratch
     pairs, slabs = compact.shape[1], near[0].shape[0] // 2
     share = pairs // N_OCC
@@ -142,7 +86,7 @@
     units = amp_ref.shape[0]
     per_step, across_units = units // STEPS, width // LANES
     depth = (units // across_units) * 8 // N_OCC
-    offsets, sizes = chunk_rows(fine * CHUNKS)
+    block = fine * CHUNKS
 
     occ, vir = lax.axis_index("occ"), lax.axis_index("vir")
     level = (vir // inner) % 2
@@ -173,7 +117,6 @@
     lax.fori_loop(1, slabs, greet, 0)
     for peer in (up, down, inside, across):
         pl.semaphore_signal(barrier, inc=1, device_id=peer, device_id_type=MESH)
-    pl.semaphore_wait(barrier, slabs - 1 + 4)
 
     def make(src, dst, sems, at, peer):
         return pltpu.make_async_remote_copy(
@@ -181,11 +124,34 @@
             device_id_type=MESH,
         )
 
-    def span(c):
-        return pl.ds(offsets[c], sizes[c])
-
-    def away_of(c):
-        return away.at[c] if c == 0 else away.at[c, :, pl.ds(0, sizes[c])]
+    def turn_over():
+        span = 8 * block
+        for n in range(ints_ref.shape[1] // span):
+            at = slice(n * span, (n + 1) * span)
+            turned[n * block : (n + 1) * block, :, 0 : ints_ref.shape[0]] = ints_ref[:, at].T.reshape(block, 8, ints_ref.shape[0])
+
+    def pack(c):
+        low_lane = lax.broadcasted_iota(jnp.int32, (fine, LANES), 1) < LANES // 2
+
+        def one_owner(w, _):
+            one, two = first_ref[w], second_ref[w]
+            left, right = turned[one * CHUNKS + c], turned[two * CHUNKS + c]
+            packed[c][w, 0:fine] = left[:, 0:LANES]
+            packed[c][w, fine : 2 * fine] = right[:, 0:LANES]
+            packed[c][w, 2 * fine : rows] = jnp.where(
+                low_lane, left[:, LANES : 2 * LANES], pltpu.roll(right[:, LANES : 2 * LANES], LANES // 2, 1)
+            )
+            if c == 0:
+                packed[c][w, rows : rows + 1] = evir_ref[one]
+                packed[c][w, rows + 1 : rows + 2] = evir_ref[two]
+                packed[c][w, rows + 2 : rows + 8] = jnp.zeros((6, LANES), jnp.float32)
+            return 0
+
+        lax.fori_loop(0, 2 * slabs, one_owner, 0)
+
+    turn_over()
+    pack(0)
+    pl.semaphore_wait(barrier, slabs - 1 + 4)
 
     panel_sems = (panel_send, panel_recv)
     panel_copies = []
@@ -263,21 +229,21 @@
     def scatter(c):
         def one(n, _):
             q = lax.rem(plane + n, slabs)
-            make(packed_ref.at[level, q, span(c)], near[c].at[plane], (xy_send, xy_recv), 2 * c, member(q)).start()
-            make(packed_ref.at[1 - level, q, span(c)], away_of(c).at[plane], (xy_send, xy_recv), 2 * c + 1,
+            make(packed[c].at[level * slabs + q], near[c].at[plane], (xy_send, xy_recv), 2 * c, member(q)).start()
+            make(packed[c].at[(1 - level) * slabs + q], away[c].at[plane], (xy_send, xy_recv), 2 * c + 1,
                  member(q)).start()
             return 0
 
         lax.fori_loop(1, slabs, one, 0)
         own_of(c, 0).start()
         own_of(c, 1).start()
+        if c + 1 < CHUNKS:
+            pack(c + 1)
 
     def own_of(c, which):
         if which == 0:
-            return pltpu.make_async_copy(packed_ref.at[level, plane, span(c)], near[c].at[plane], own_sem.at[1 + 2 * c])
-        return pltpu.make_async_copy(
-            packed_ref.at[1 - level, plane, span(c)], away_of(c).at[plane], own_sem.at[2 + 2 * c]
-        )
+            return pltpu.make_async_copy(packed[c].at[level * slabs + plane], near[c].at[plane], own_sem.at[1 + 2 * c])
+        return pltpu.make_async_copy(packed[c].at[(1 - level) * slabs + plane], away[c].at[plane], own_sem.at[2 + 2 * c])
 
     def whole(ref, count, sem):
         at = ref.at[pl.ds(0, count)]
@@ -285,7 +251,7 @@
 
     def flips(c):
         count = slabs // 2
-        source = away_of(c)
+        source = away[c]
         return [
             make(source.at[pl.ds(n * count, count)], near[c].at[pl.ds(slabs + n * count, count)],
                  (flip_send, flip_recv), 2 * c + n, peer)
@@ -312,7 +278,7 @@
         return make(result.at[c, 1], out_ref.at[c, group(-2)], sems, at, up)
 
     def gather(c):
-        whole(away_of(c), slabs - 1, xy_recv.at[2 * c + 1]).wait()
+        whole(away[c], slabs - 1, xy_recv.at[2 * c + 1]).wait()
         own_of(c, 1).wait()
         for copy in flips(c):
             copy.start()
@@ -433,17 +399,19 @@
         for copy in flips(c):
             copy.wait_send()
         whole(near[c], slabs - 1, xy_send.at[2 * c]).wait()
-        whole(away_of(c), slabs - 1, xy_send.at[2 * c + 1]).wait()
+        whole(away[c], slabs - 1, xy_send.at[2 * c + 1]).wait()
     for copy in panel_copies + energy_copies:
         copy.wait_send()
 
 
-def ladder_of(packed, amplitudes, eps_occ, panel_owner, slot_of, digits):
-    _, slabs, total_rows, lanes = packed.shape
+def ladder_of(integrals, energies, amplitudes, eps_occ, panel_owner, slot_of, first, second, digits):
+    blocks, lanes = energies.shape
+    depth, col_count = integrals.shape
+    slabs = first.shape[0] // 2
     pairs = slot_of.shape[0]
     panel_rows, width = amplitudes.shape
     share = pairs // N_OCC
-    _, sizes = chunk_rows((total_rows - 8) // 3)
+    sizes = chunk_rows(col_count // blocks)
     rows = sizes[-1]
     fine = rows // 3
     f32, bf16 = jnp.float32, jnp.bfloat16
@@ -460,13 +428,13 @@
     return pl.pallas_call(
         functools.partial(ladder_kernel, digits),
         out_shape=jax.ShapeDtypeStruct((CHUNKS, pairs, 2 * fine, width), f32),
-        in_specs=[smem, smem, pl.BlockSpec(memory_space=pl.ANY), vmem, vmem],
+        in_specs=[smem] * 4 + [vmem] * 4,
         out_specs=vmem,
-        scratch_shapes=[pltpu.VMEM((2 * slabs, size, lanes), f32) for size in sizes]
+        scratch_shapes=[pltpu.VMEM((count_of, size, lanes), f32) for count_of in (2 * slabs, slabs, 2 * slabs) for size in sizes]
         + arrived
         + kept[:-1]
         + [
-            pltpu.VMEM((CHUNKS, slabs, sizes[0], lanes), f32),
+            pltpu.VMEM((col_count // 8, 8, 2 * lanes), f32),
             pltpu.VMEM((CHUNKS, pairs, rows, lanes), f32),
             pltpu.VMEM((CHUNKS, 2, N_OCC, share, rows, lanes), f32),
             pltpu.VMEM((CHUNKS, 2, share, 2 * fine, width), f32),
@@ -488,9 +456,9 @@
             dma((count,)),
             dma((count,)),
         ],
-        compiler_params=pltpu.CompilerParams(collective_id=1, has_side_effects=True, vmem_limit_bytes=60 * 2**20),
+        compiler_params=pltpu.CompilerParams(collective_id=1, has_side_effects=True, vmem_limit_bytes=63 * 2**20),
         name="ladder",
-    )(slot_of, panel_owner, packed, amps, eps_occ[None, :])
+    )(slot_of, panel_owner, first, second, integrals, energies[:, None], amps, eps_occ[None, :])
 
 
 def local(amplitudes, integrals, eps_vir, eps_occ, panel_owner, block_target):
@@ -527,9 +495,9 @@
     source = jnp.sum(jnp.where(found, stands[None], 0), axis=(1, 2))
 
     energies = jnp.pad(eps_vir.reshape(blocks_dev, block), ((0, 0), (0, LANES - block)))
-    packed = pack(integrals, energies, first, second)
-    packed = packed.reshape(levels, slabs, packed.shape[1], LANES)
-    ladder = ladder_of(packed, amplitudes, eps_occ, panel_owner, slot_of, DIGITS)
+    ladder = ladder_of(
+        integrals, energies, amplitudes, eps_occ, panel_owner, slot_of, first, second, DIGITS
+    )
     return place(ladder, source)
 
 

time: 306 us -> 301 us (0.984)
  Pallas kernels: 300 us -> 293 us
    pallas_call x1 -> x0, Pallas kernels: 9.1 us -> none  [pack(): pl.pallas_call(pack_kernel, out_shape=jax.ShapeDtypeStruct((dests, rows,...]
where the time goes in v6:
time: 301 us; the launch traced here: 299 us
  Pallas kernels  293 us (97%)
  other arithmetic  3.79 us (1%)
    pallas_call x1, Pallas kernels, ladder_of(): pl.pallas_call(functools.partial(ladder_kernel, digits), out_shape=jax.Sh...  286 us
    pallas_call x1, Pallas kernels, place(): pl.pallas_call(place_kernel, out_shape=jax.ShapeDtypeStruct((blocks * blo...  6.93 us

profile of v6, /device:TPU:1, one launch (start us, length us, event | category | flops | bytes accessed | tf_op | source)
XLA Modules:
  0.0 298.6 jit_solution(7292932983229093014)
XLA Ops:
  0.0 0.8 eq.70
  0.8 0.8 reshape.190
  1.6 0.6 pad.4
  2.2 0.1 fusion.13
  2.4 0.2 select_reduce_fusion.1
  2.6 0.7 select_reduce_fusion.2.slot_ref
  3.3 0.8 fusion.1
  4.0 0.1 convert_add_fusion
  4.1 1.9 select_reduce_fusion.source_ref
  6.0 285.6 %ladder.1.ladder_ref = f32[10,32,16,256]{3,2,1,0:T(8,128)} custom-call(s32[32]{0:T(128)} %select_reduce_fusion.2.slot_ref, s32[12]{0:T(128)} %owner_ref.1, s32[64]{0:T(128)} %get-tuple-element.6.first_ref, s32[64]{0:T(128)} %get-tuple-element.5.second_ref, f32[192,5120]{1,0:T(8,128)} %ints_ref.1, f32[64,1,128]{2,1,0:T(1,128)} %bitcast.10, ...), custom_call_target="tpu_custom_call" | custom-call | tf_op jit(solution)/shard_map/ladder/pallas_call | solution.py:428
  291.7 6.9 %place.1 = f32[5120,256]{1,0:T(8,128)} custom-call(s32[64]{0:T(128)} %select_reduce_fusion.source_ref, f32[10,32,16,256]{3,2,1,0:T(8,128)} %ladder.1.ladder_ref), custom_call_target="tpu_custom_call" | custom-call | tf_op jit(solution)/shard_map/place/pallas_call | solution.py:57
  (5 shorter events, 0.0 us)
